TPU v7x, 32 devices: a whole 2x2x4 slice. The times are simulated.
32 devices in a mesh: obs: 8 (over z, y), lvl: 4 (over x, core).
Axes of the slice: x: 2, y: 2, z: 4, core: 2. Of those that a mesh axis runs over, the one named last changes fastest.
Arguments:
- rhs: float32 [64, 262144], P(None, ('obs', 'lvl')), may hold values from -15 to 15
- tile_weights: bfloat16 [4096, 64, 128], P(('obs', 'lvl')), may hold values from -0.3125 to 0.3125
- tile_owner: int32 [4096, 1], P(('obs', 'lvl')), may hold values from 0 to 31; in each aligned block of 128 rows (0 to 127, 128 to 255, ...) at most 8 rows name the same one
- tile_row: int32 [4096], P(('obs', 'lvl')), may hold values from 0 to 31
- axis_a: bfloat16 [128, 8, 128], P('obs', 'lvl'), as said below
- axis_b: bfloat16 [8, 128, 128], P('lvl'), as said below
- coupling: float32 [8, 8], replicated, as said below
- noise: float32 [64], replicated, may hold values from 0.1 to 1
Outputs:
- solution: float32 [64, 262144], P(None, ('obs', 'lvl'))
- residual: float32 [64, 262144], P(None, ('obs', 'lvl'))
Inputs may be any that keep to these rules, and one draw needn't show every extreme that they name: `tile_owner`: among the 128 tiles of one device no owner is named more than 8 times, a bound that some block reaches. For each level l, axis_a[x, l, a] equals axis_a[a, l, x]. For each level l, axis_b[l] is symmetric. coupling is symmetric and positive definite.
All inputs are finite; a program needn't handle non-finite values.
Results may differ from a plain program's by a relative error of at most 0.017.
Values may be sent and summed in bfloat16 or wider, within the bound.
No kernel may reach another device: no remote copies, remote signals or barrier semaphores. Data moves between devices by JAX's collectives and lax.ppermute only.
A program may use at most 64 MiB of HBM per device.

v0:
```python
import jax
import jax.numpy as jnp
from jax import lax
from jax.sharding import PartitionSpec as P

ITERS = 2


def on_device(rhs, tile_weights, tile_owner, tile_row, axis_a, axis_b, coupling, noise):
    devices = lax.axis_size(("obs", "lvl"))
    obs_count = lax.axis_size("obs")
    lvl_count = lax.axis_size("lvl")
    tile_count, tile_obs, node_cols = tile_weights.shape
    columns = rhs.shape[0]
    a_rows, lvl_here, grid_first = axis_a.shape
    capacity = max(2, 2 * tile_count // devices)
    owner = tile_owner[:, 0]
    my_coupling = lax.dynamic_slice_in_dim(coupling, lax.axis_index("lvl") * lvl_here, lvl_here, 0)
    col_width = columns // obs_count
    lvl_cap = obs_count * capacity
    lvl_slots = lvl_count * lvl_cap
    whole_rows = grid_first * lvl_here
    whole_kernel = lax.all_gather(axis_a, "obs", axis=0, tiled=True)
    level_of = owner % lvl_count
    lvl_hits = (level_of[:, None] == jnp.arange(lvl_count, dtype=jnp.int32)[None, :]).astype(
        jnp.int32
    )
    lvl_before = jnp.cumsum(lvl_hits, axis=0) - lvl_hits
    lvl_position = jnp.sum(lvl_before * lvl_hits, axis=1)
    lvl_slot = level_of * lvl_cap + lvl_position
    first_index = owner // lvl_count * a_rows + tile_row // lvl_here
    target = first_index * lvl_here + tile_row % lvl_here
    target_out = jnp.zeros((lvl_slots,), jnp.int32).at[lvl_slot].set(target)
    target_out = jnp.broadcast_to(target_out[None, :], (obs_count, lvl_slots)).reshape(
        devices, lvl_cap
    )
    col_rows = lax.all_to_all(
        target_out, ("obs", "lvl"), split_axis=0, concat_axis=0, tiled=True
    ).reshape(devices * lvl_cap)
    col_collect = (jnp.arange(whole_rows, dtype=jnp.int32)[:, None] == col_rows[None, :]).astype(
        jnp.bfloat16
    )

    def local_axes(field):
        first = jnp.einsum(
            "alrb,lbc->alrc", field, axis_b, preferred_element_type=jnp.float32
        ).astype(jnp.bfloat16)
        return jnp.einsum(
            "xla,alrc->xlrc", whole_kernel, first, preferred_element_type=jnp.float32
        ).astype(jnp.bfloat16)

    def squared_norm(field):
        return lax.psum(jnp.sum(field * field, axis=1), ("obs", "lvl"))

    solution = jnp.zeros_like(rhs)
    residual = rhs
    direction = rhs
    norm_now = squared_norm(residual)
    for step in range(ITERS):
        low = direction.astype(jnp.bfloat16).reshape(obs_count, col_width, tile_count, tile_obs)
        part = jnp.einsum(
            "jckt,ktn->jkcn", low, tile_weights, preferred_element_type=jnp.float32
        ).astype(jnp.bfloat16)
        outgoing = (
            jnp.zeros((obs_count, lvl_slots, col_width, node_cols), jnp.bfloat16)
            .at[:, lvl_slot]
            .set(part)
        )
        outgoing = outgoing.reshape(devices, lvl_cap, col_width, node_cols)
        received = lax.all_to_all(outgoing, ("obs", "lvl"), split_axis=0, concat_axis=0, tiled=True)
        width = received.shape[2]
        flat = received.reshape(devices * lvl_cap, width * node_cols)
        summed = jnp.dot(col_collect, flat, preferred_element_type=jnp.float32)
        node_sums = summed.reshape(whole_rows, width, node_cols).astype(jnp.bfloat16)
        grid = node_sums.reshape(grid_first, lvl_here, col_width, node_cols)
        grid_values = local_axes(
            jnp.einsum(
                "lm,amrc->alrc",
                my_coupling,
                lax.all_gather(local_axes(grid), "lvl", axis=1, tiled=True).astype(jnp.float32),
                precision=lax.Precision.HIGHEST,
            ).astype(jnp.bfloat16)
        ).reshape(whole_rows, col_width, node_cols)
        returning = grid_values[col_rows].reshape(devices, lvl_cap, col_width, node_cols)
        spread_received = lax.all_to_all(
            returning, ("obs", "lvl"), split_axis=0, concat_axis=0, tiled=True
        )
        spread_width = spread_received.shape[2]
        mine = spread_received.reshape(obs_count, lvl_slots, spread_width, node_cols)[:, lvl_slot]
        values = jnp.einsum(
            "jkcn,ktn->jckt", mine, tile_weights, preferred_element_type=jnp.float32
        )
        back = values.astype(jnp.bfloat16).reshape(obs_count, spread_width, tile_count * tile_obs)
        back = back.reshape(columns, tile_count * tile_obs)
        image = back.astype(jnp.float32) + noise[:, None] * direction
        alpha = norm_now / lax.psum(jnp.sum(direction * image, axis=1), ("obs", "lvl"))
        solution = solution + alpha[:, None] * direction
        residual = residual - alpha[:, None] * image
        if step + 1 < ITERS:
            norm_next = squared_norm(residual)
            direction = residual + (norm_next / norm_now)[:, None] * direction
            norm_now = norm_next
    return (solution, residual)


def solution(mesh):
    in_specs = (
        P(None, ("obs", "lvl")),
        P(("obs", "lvl"), None, None),
        P(("obs", "lvl"), None),
        P(("obs", "lvl")),
        P("obs", "lvl", None),
        P("lvl", None, None),
        P(),
        P(),
    )
    out_specs = (P(None, ("obs", "lvl")), P(None, ("obs", "lvl")))
    return jax.shard_map(
        on_device, mesh=mesh, in_specs=in_specs, out_specs=out_specs, check_vma=False
    )
```

profile of v0, /device:TPU:0, one launch (start us, length us, event | category | flops | bytes accessed | tf_op | source)
XLA Modules:
  0.0 783.8 jit_solution(10749742088833965640)
XLA Ops:
  7.2 0.8 fusion.98
  9.8 1.0 scatter_custom_fusion
  11.5 7.3 all-to-all-start
  18.8 1.7 convert_element_type.117
  20.5 3.3 reshape.101
  23.8 4.6 fusion.33
  28.3 2.5 broadcast.71.clone
  30.9 17.6 %scatter_fusion = bf16[8,256,8,128]{3,2,1,0:T(8,128)(2,1)} fusion(bf16[8,256,8,128]{3,2,1,0:T(8,128)(2,1)} %broadcast.71.clone, s32[128]{0:T(128)S(1)} %fusion.89, bf16[128,8,8,128]{3,2,1,0:T(8,128)(2,1)} %fusion.33), kind=kCustom, calls=%fused_computation.5 | custom fusion | bytes 6291968 | tf_op jit(solution)/shard_map/scatter | solution.py:67
  48.5 6.0 all-to-all-start.1
  54.5 113.5 %all_gather.9 = bf16[128,2,128]{2,0,1:T(8,128)(2,1)S(1)} all-gather(bf16[16,2,128]{2,0,1:T(8,128)(2,1)S(1)} %copy.25), channel_id=1, replica_groups=mesh['obs'=8,'lvl'=4] {'obs'}, dimensions={0}, use_global_device_ids=true | all-gather | bytes 73728 | tf_op jit(solution)/shard_map/all_gather | solution.py:23
  169.3 5.3 copy.86
  174.6 6.5 copy.23
  181.0 3.5 fusion.36
  185.3 1.1 copy.27
  186.6 21.7 %all-gather.3.cloned.1.call-done = bf16[128,8,8,128]{3,2,0,1:T(8,128)(2,1)} async-done(((bf16[128,2,8,128]{3,2,0,1:T(8,128)(2,1)}), bf16[128,8,8,128]{3,2,0,1:T(8,128)(2,1)}) %all-gather.3.cloned.1.call-update) | async-done | bytes 2097168 | tf_op jit(solution)/shard_map/all_gather | solution.py:80
  208.2 4.1 fusion.59
  213.2 14.6 %gather_fusion = bf16[2048,8,128]{2,1,0:T(8,128)(2,1)} fusion(bf16[256,8,128]{2,1,0:T(8,128)(2,1)S(1)} %bitcast.170, s32[2048]{0:T(1024)S(1)} %broadcast_clamp_fusion), kind=kCustom, calls=%fused_computation | custom fusion | bytes 8396800 | tf_op jit(solution)/shard_map/gather | solution.py:84
  227.8 4.7 all-to-all-start.2
  232.8 93.5 %all-to-all-done.2 = bf16[32,64,8,128]{3,2,1,0:T(8,128)(2,1)} async-done(((bf16[32,64,8,128]{3,2,1,0:T(8,128)(2,1)}), bf16[32,64,8,128]{3,2,1,0:T(8,128)(2,1)}, u32[]{:S(2)}, u32[]{:S(2)}) %all-to-all-start.2) | async-done | bytes 4194336 | tf_op jit(solution)/shard_map/all_to_all | solution.py:85
  326.3 4.7 gather_fusion.1
  331.0 2.8 convert_bitcast_fusion.1
  333.8 4.4 copy.31
  338.1 4.8 reshape.116
  342.9 2.8 multiply_reduce_fusion.2
  345.7 38.2 %all-reduce = (f32[64]{0:T(128)S(1)}, f32[64]{0:T(128)S(1)}) all-reduce(f32[64]{0:T(128)S(1)} %get-tuple-element.3, f32[64]{0:T(128)S(1)} %get-tuple-element.2), channel_id=1, replica_groups=mesh['obs'=8,'lvl'=4] {'obs','lvl'}, use_global_device_ids=true, to_apply=%region_1.2 | all-reduce | flops 128 | bytes 1024 | tf_op jit(solution)/shard_map/psum | solution.py:53
  383.8 2.8 multiply_reduce_fusion.1
  386.6 40.9 %psum.30 = f32[64]{0:T(128)S(1)} all-reduce(f32[64]{0:T(128)S(1)} %multiply_reduce_fusion.1), channel_id=1, replica_groups=mesh['obs'=8,'lvl'=4] {'obs','lvl'}, use_global_device_ids=true, to_apply=%region_9.10 | all-reduce | flops 64 | bytes 512 | tf_op jit(solution)/shard_map/psum | solution.py:53
  427.5 2.7 fusion.94
  430.3 3.3 reshape.109
  433.5 4.6 fusion.24
  438.1 2.5 broadcast.71
  440.6 17.6 %scatter_fusion.1 = bf16[8,256,8,128]{3,2,1,0:T(8,128)(2,1)} fusion(bf16[8,256,8,128]{3,2,1,0:T(8,128)(2,1)} %broadcast.71, s32[128]{0:T(128)S(1)} %fusion.89, bf16[128,8,8,128]{3,2,1,0:T(8,128)(2,1)} %fusion.24), kind=kCustom, calls=%fused_computation.6 | custom fusion | bytes 6291968 | tf_op jit(solution)/shard_map/scatter | solution.py:67
  458.2 98.8 %all_to_all.29 = bf16[32,64,8,128]{3,2,1,0:T(8,128)(2,1)S(1)} all-to-all(bf16[32,64,8,128]{3,2,1,0:T(8,128)(2,1)} %bitcast.171), channel_id=1, replica_groups=mesh['obs'=8,'lvl'=4] {'obs','lvl'}, dimensions={0} | all-to-all | bytes 8388608 | tf_op jit(solution)/shard_map/all_to_all | solution.py:70
  557.1 3.0 copy.85
  560.1 6.5 copy.33
  566.6 3.5 fusion.39
  570.8 1.1 copy.36
  571.9 21.8 %all-gather.5.cloned.1.call-done = bf16[128,8,8,128]{3,2,0,1:T(8,128)(2,1)} async-done(((bf16[128,2,8,128]{3,2,0,1:T(8,128)(2,1)}), bf16[128,8,8,128]{3,2,0,1:T(8,128)(2,1)}) %all-gather.5.cloned.1.call-update) | async-done | bytes 2097168 | tf_op jit(solution)/shard_map/all_gather | solution.py:80
  593.7 4.1 fusion.56
  598.7 14.7 %gather_fusion.2 = bf16[2048,8,128]{2,1,0:T(8,128)(2,1)} fusion(bf16[256,8,128]{2,1,0:T(8,128)(2,1)S(1)} %bitcast.169, s32[2048]{0:T(1024)S(1)} %broadcast_clamp_fusion), kind=kCustom, calls=%fused_computation.2 | custom fusion | bytes 8396800 | tf_op jit(solution)/shard_map/gather | solution.py:84
  613.4 98.6 %all_to_all.30 = bf16[32,64,8,128]{3,2,1,0:T(8,128)(2,1)} all-to-all(bf16[32,64,8,128]{3,2,1,0:T(8,128)(2,1)} %bitcast.173), channel_id=1, replica_groups=mesh['obs'=8,'lvl'=4] {'obs','lvl'}, dimensions={0} | all-to-all | bytes 8388608 | tf_op jit(solution)/shard_map/all_to_all | solution.py:85
  711.9 4.7 gather_fusion.3
  716.6 2.8 convert_bitcast_fusion
  719.4 4.4 copy.40
  723.8 4.8 reshape.117
  728.6 3.7 multiply_reduce_fusion
  732.3 38.5 %psum.31 = f32[64]{0:T(128)S(1)} all-reduce(f32[64]{0:T(128)S(1)} %multiply_reduce_fusion), channel_id=1, replica_groups=mesh['obs'=8,'lvl'=4] {'obs','lvl'}, use_global_device_ids=true, to_apply=%region_12.13 | all-reduce | flops 64 | bytes 512 | tf_op jit(solution)/shard_map/psum | solution.py:96
  770.8 5.8 multiply_subtract_fusion
  (42 shorter events, 7.4 us)
Async XLA Ops:
  7.2 16.6 %copy-start = (bf16[128,64,128]{2,1,0:T(8,128)(2,1)S(1)}, bf16[128,64,128]{2,1,0:T(8,128)(2,1)}, u32[]{:S(2)}) copy-start(bf16[128,64,128]{2,1,0:T(8,128)(2,1)} %param.9) | copy-start | bytes 6291460
  11.5 37.0 %all-to-all-start = ((s32[32,1,64]{2,1,0:T(1,128)}), s32[32,1,64]{2,1,0:T(1,128)S(1)}, u32[]{:S(2)}, u32[]{:S(2)}) async-start(s32[32,1,64]{2,1,0:T(1,128)} %bitcast.4), calls=%async_computation | async-start | bytes 32768 | tf_op jit(solution)/shard_map/all_to_all | solution.py:37
  48.5 6.0 copy-start.3
  48.5 120.8 %all-to-all-start.1 = ((bf16[32,64,8,128]{3,2,1,0:T(8,128)(2,1)}), bf16[32,64,8,128]{3,2,1,0:T(8,128)(2,1)}, u32[]{:S(2)}, u32[]{:S(2)}) async-start(bf16[32,64,8,128]{3,2,1,0:T(8,128)(2,1)} %bitcast.168), calls=%async_computation.1 | async-start | bytes 8388608 | tf_op jit(solution)/shard_map/all_to_all | solution.py:70
  54.5 153.8 %all-gather.3.cloned.1.call-start = ((), (), s32[]{:S(2)}) async-start(), calls=%async_computation.5 | async-start | bytes 2621440 | tf_op jit(solution)/shard_map/all_gather | solution.py:80
  181.0 3.5 copy-start.1
  184.6 23.7 %copy-start.4 = (f32[8,8]{1,0:T(8,128)S(1)}, f32[8,8]{1,0:T(8,128)}, u32[]{:S(2)}) copy-start(f32[8,8]{1,0:T(8,128)} %param.14) | copy-start | bytes 772
  227.8 98.4 %all-to-all-start.2 = ((bf16[32,64,8,128]{3,2,1,0:T(8,128)(2,1)}), bf16[32,64,8,128]{3,2,1,0:T(8,128)(2,1)}, u32[]{:S(2)}, u32[]{:S(2)}) async-start(bf16[32,64,8,128]{3,2,1,0:T(8,128)(2,1)} %bitcast.172), calls=%async_computation.2 | async-start | bytes 8388608 | tf_op jit(solution)/shard_map/all_to_all | solution.py:85
  232.6 361.2 %all-gather.5.cloned.1.call-start = ((), (), s32[]{:S(2)}) async-start(), calls=%async_computation.6 | async-start | bytes 2621440 | tf_op jit(solution)/shard_map/all_gather | solution.py:80
  338.1 4.8 copy-start.2
Sparse Core Ops, SparseCore 0:
  186.6 21.6 all-gather.2
  572.1 21.6 all-gather.4
where the time goes:
time: 789 us; the launch traced here: 784 us
  blocking collectives  429 us (54%)
  waiting for transfers between devices  137 us (17%)
  local copies, waits for them, and re-layouts  130 us (16%)
  matrix products  32.4 us (4%)
  other arithmetic  22.9 us (3%)
  starting transfers between devices  18.3 us (2%)
  between operations  14.5 us (2%)
    all_gather x1, blocking collectives, on_device(): whole_kernel = lax.all_gather(axis_a, 'obs', axis=0, tiled=True)  113 us
    all_to_all x1, blocking collectives, on_device(): lax.all_to_all(outgoing, ('obs', 'lvl'), split_axis=0, concat_axis=0, til...  98.8 us
    all_to_all x1, blocking collectives, on_device(): lax.all_to_all(returning, ('obs', 'lvl'), split_axis=0, concat_axis=0, ti...  98.6 us
    all_to_all x1, waiting for transfers between devices, on_device(): lax.all_to_all(returning, ('obs', 'lvl'), split_axis=0, concat_axis=0, ti...  93.5 us
    psum x2, blocking collectives, squared_norm(): return lax.psum(jnp.sum(field * field, axis=1), ('obs', 'lvl'))  79.1 us
    all_gather x2, waiting for transfers between devices, on_device(): lax.all_gather(local_axes(grid), 'lvl', axis=1, tiled=True)  43.5 us
    psum x1, blocking collectives, on_device(): lax.psum(jnp.sum(direction * image, axis=1), ('obs', 'lvl'))  38.5 us
    scatter x2, local copies, waits for them, and re-layouts, on_device(): outgoing = jnp.zeros((obs_count, lvl_slots, col_width, node_cols), jnp.bf...  35.2 us
  transfers between devices with their start and end apart: 5, of which 3 were waited for; matrix products, arithmetic and copies ran while one was open for 4% of the time, Pallas kernels for 0%

commit v1 on v0

v1 whole, which is shorter than its diff:
```python
import jax
import jax.numpy as jnp
from jax import lax
from jax.experimental import pallas as pl
from jax.experimental.pallas import tpu as pltpu
from jax.sharding import Mesh
from jax.sharding import PartitionSpec as P


SPLIT = ("half", "part", "lvl")
PEERS = ("part", "lvl")
F32 = jnp.float32
BF16 = jnp.bfloat16
EXTRA = 16
BLOCK = 16
SCALARS = 8
UNROLL = 8
BASE = 128


def pieces(value):
    high = value.astype(BF16).astype(F32)
    rest = value - high
    middle = rest.astype(BF16).astype(F32)
    return high, middle, rest - middle


def pair_weights(weights_ref, k):
    pair = weights_ref[pl.ds(2 * k, 2)]
    zero = jnp.zeros_like(pair[0])
    return jnp.concatenate(
        [jnp.concatenate([pair[0], zero], 1), jnp.concatenate([zero, pair[1]], 1)], 0
    )


class Plan:
    def __init__(self, devices, columns, tiles, tile_obs, nodes, extra):
        self.devices, self.columns, self.tiles = devices, columns, tiles
        self.tile_obs, self.nodes = tile_obs, nodes
        self.mine = columns // devices
        self.data = self.mine * tiles
        self.rows = self.data + extra

    def rows_of(self, first):
        return pl.ds(first, self.devices, stride=self.rows)


def put_parts(plan, scratch, low, weights2, k):
    part = jnp.dot(low, weights2, preferred_element_type=F32)
    for c in range(plan.mine):
        rows = part[c * plan.devices : (c + 1) * plan.devices]
        for h in range(2):
            scratch[plan.rows_of(c * plan.tiles + 2 * k + h), :] = rows[
                :, h * plan.nodes : (h + 1) * plan.nodes
            ]


def put_sums(plan, scratch, sums):
    row = plan.data
    for value in sums:
        total = jnp.sum(value, axis=1, keepdims=True)
        total = jnp.broadcast_to(total, (plan.columns, plan.nodes))
        for c in range(plan.mine):
            for piece in pieces(total[c * plan.devices : (c + 1) * plan.devices]):
                scratch[plan.rows_of(row), :] = piece
                row += 1
    while row < plan.data + EXTRA:
        scratch[plan.rows_of(row), :] = jnp.zeros((plan.devices, plan.nodes), F32)
        row += 1


def write_out(plan, scratch, out_ref, setup=()):
    live = plan.data + EXTRA

    def cast(d, unused):
        rows = pl.ds(pl.multiple_of(d * plan.rows, 8), live)
        out_ref[d, :live] = scratch[rows, :].astype(BF16)
        row = live
        for block in setup:
            out_ref[d, row : row + block.shape[0]] = block
            row += block.shape[0]
        return unused

    lax.fori_loop(0, plan.devices, cast, 0, unroll=2)


def send_kernel(plan, low_ref, weights_ref, *refs):
    block = 2 * plan.tile_obs
    *setup_refs, out_ref, scratch = refs

    def step(k, total):
        field = low_ref[:, pl.ds(pl.multiple_of(k * block, block), block)]
        put_parts(plan, scratch, field.astype(BF16), pair_weights(weights_ref, k), k)
        return total + field * field

    total = lax.fori_loop(
        0, plan.tiles // 2, step, jnp.zeros((plan.columns, block), F32), unroll=UNROLL
    )
    put_sums(plan, scratch, [total])
    write_out(plan, scratch, out_ref, [ref[...] for ref in setup_refs])


def joined(plan, received_ref, source):
    return jnp.concatenate(
        [received_ref[source, c * plan.tiles : (c + 1) * plan.tiles] for c in range(plan.mine)], 1
    )


def owner_sum(plan, received_ref, first):
    sums = jnp.sum(received_ref[:, plan.data : plan.data + EXTRA].astype(F32), axis=0)
    return [
        sums[first + 3 * c : first + 3 * c + 1]
        + sums[first + 3 * c + 1 : first + 3 * c + 2]
        + sums[first + 3 * c + 2 : first + 3 * c + 3]
        for c in range(plan.mine)
    ]


def collect(plan, received_ref, index_ref, acc_ref):
    node_count = acc_ref.shape[0]
    acc_ref[...] = jnp.zeros_like(acc_ref)

    def step(j, unused):
        hots = []
        for h in range(2):
            index = index_ref[pl.ds(2 * j + h, 1), :]
            nodes = lax.broadcasted_iota(jnp.int32, (node_count, plan.tiles), 0)
            hots.append(jnp.where(nodes == index, 1.0, 0.0).astype(BF16))
        data = jnp.concatenate([joined(plan, received_ref, 2 * j + h) for h in range(2)], 0)
        acc_ref[...] += jnp.dot(jnp.concatenate(hots, 1), data, preferred_element_type=F32)
        return unused

    lax.fori_loop(0, plan.devices // 2, step, 0)


def grid_steps(plan, levels, sums_ref, axis_a_ref, axis_b_ref, coupling_ref, spread_ref, grid_ref):
    first = axis_a_ref.shape[1]

    def axes(field, l):
        steps = jnp.concatenate(
            [
                jnp.dot(
                    field[:, c * plan.nodes : (c + 1) * plan.nodes],
                    axis_b_ref[l],
                    preferred_element_type=F32,
                ).astype(BF16)
                for c in range(plan.mine)
            ],
            1,
        )
        return jnp.dot(axis_a_ref[l], steps, preferred_element_type=F32)

    for l in range(levels):
        field = sums_ref[l * first : (l + 1) * first]
        spread_ref[l] = axes(field, l).astype(BF16).astype(F32)
    for l in range(levels):
        mixed = coupling_ref[l, 0] * spread_ref[0]
        for m in range(1, levels):
            mixed = mixed + coupling_ref[l, m] * spread_ref[m]
        grid_ref[l * first : (l + 1) * first] = axes(mixed.astype(BF16), l).astype(BF16)


def products(plan, sums_ref, grid_ref):
    total = jnp.sum(sums_ref[...].astype(F32) * grid_ref[...].astype(F32), axis=0, keepdims=True)
    return [
        jnp.sum(total[:, c * plan.nodes : (c + 1) * plan.nodes], axis=1, keepdims=True)
        for c in range(plan.mine)
    ]


def give_back(plan, grid_ref, index_t_ref, out_ref, scalars):
    node_count = grid_ref.shape[0]
    group = 4

    rows = []
    for value in scalars:
        rows += list(pieces(jnp.broadcast_to(value, (1, plan.nodes))))
    rows.append(jnp.zeros((EXTRA - len(rows), plan.nodes), F32))
    extra = jnp.concatenate(rows, 0).astype(BF16)
    for j in range(plan.devices // group):
        hots = []
        for h in range(group):
            index = index_t_ref[:, j * group + h : j * group + h + 1]
            nodes = lax.broadcasted_iota(jnp.int32, (plan.tiles, node_count), 1)
            hots.append(jnp.where(nodes == index, 1.0, 0.0).astype(BF16))
        picked = jnp.dot(
            jnp.concatenate(hots, 0), grid_ref[...], preferred_element_type=F32
        ).astype(BF16)
        for h in range(group):
            for c in range(plan.mine):
                out_ref[j * group + h, c * plan.tiles : (c + 1) * plan.tiles] = picked[
                    h * plan.tiles : (h + 1) * plan.tiles, c * plan.nodes : (c + 1) * plan.nodes
                ]
            out_ref[j * group + h, plan.data : plan.data + EXTRA] = extra


def read_setup(
    plan, part, lvl, a_rows, lvl_here, b_rows, received_ref, axis_a_ref, axis_b_ref, index_ref,
    index_t_ref,
):
    base = plan.data + EXTRA
    for o in range(part):
        for v in range(lvl):
            for l in range(lvl_here):
                row = base + l * a_rows
                axis_a_ref[v * lvl_here + l, o * a_rows : (o + 1) * a_rows] = received_ref[
                    o * lvl + v, row : row + a_rows
                ]
                row = base + lvl_here * a_rows + l * b_rows
                axis_b_ref[v * lvl_here + l, o * b_rows : (o + 1) * b_rows] = received_ref[
                    o * lvl + v, row : row + b_rows
                ]
    row = base + lvl_here * (a_rows + b_rows)
    for d in range(plan.devices):
        split = received_ref[d, row : row + 8].astype(F32)
        index_ref[d : d + 1] = (split[0:1] * float(BASE) + split[1:2]).astype(jnp.int32)
    square = index_ref[...].astype(F32)
    square = jnp.concatenate(
        [square] + [jnp.zeros((plan.tiles - plan.devices, plan.tiles), F32)], 0
    )
    index_t_ref[...] = square.T.astype(jnp.int32)


def collect_kernel(plan, quantities, received_ref, index_ref, out_ref, acc_ref):
    collect(plan, received_ref, index_ref, acc_ref)
    node_count = acc_ref.shape[0]
    out_ref[:node_count] = acc_ref[...].astype(BF16)
    rows = []
    for q in range(quantities):
        sums = owner_sum(plan, received_ref, 3 * plan.mine * q)
        rows += list(pieces(jnp.concatenate(sums, 1)))
    rows.append(jnp.zeros((SCALARS - len(rows), plan.mine * plan.nodes), F32))
    out_ref[node_count:] = jnp.concatenate(rows, 0).astype(BF16)


def grid_kernel(
    plan, opening, start_column, coupling_ref, noise_ref, place_ref, own_ref, other_ref, own_a_ref,
    other_a_ref, axis_b_ref, index_t_ref, *refs,
):
    axis_a_ref, sums_ref, grid_ref, spread_ref = refs[-4:]
    node_count, _ = sums_ref.shape
    half = own_a_ref.shape[1]
    axis_a_ref[:, pl.ds(pl.multiple_of(place_ref[1] * half, half), half)] = own_a_ref[...]
    axis_a_ref[:, pl.ds(pl.multiple_of((1 - place_ref[1]) * half, half), half)] = other_a_ref[...]

    total = own_ref[:node_count].astype(F32) + other_ref[:node_count].astype(F32)
    rows = own_ref[node_count:].astype(F32) + other_ref[node_count:].astype(F32)
    square = rows[0:1] + rows[1:2] + rows[2:3]
    if opening:
        out_ref, kept_ref, square_ref = refs[:3]
        kept_ref[...] = total
        square_ref[...] = square
        length, beta = square, None
    else:
        kept_ref, square_ref, out_ref = refs[:3]
        cross = rows[3:4] + rows[4:5] + rows[5:6]
        old = square_ref[...]
        beta = square / old
        total = total + beta * kept_ref[...]
        length = square + beta * (2.0 * cross + beta * old)
    sums_ref[...] = total.astype(BF16)
    levels = axis_a_ref.shape[0]
    grid_steps(plan, levels, sums_ref, axis_a_ref, axis_b_ref, coupling_ref, spread_ref, grid_ref)
    quads = products(plan, sums_ref, grid_ref)
    alphas, betas = [], []
    for c in range(plan.mine):
        here = slice(c * plan.nodes, (c + 1) * plan.nodes)
        noise = noise_ref[start_column + c * plan.devices + place_ref[0]]
        alphas.append(square[:, here] / (quads[c] + noise * length[:, here]))
        if beta is not None:
            betas.append(beta[:, here])
    give_back(plan, grid_ref, index_t_ref, out_ref, alphas + betas)


def unpack(plan, received_ref, scratch):
    def cast(d, unused):
        scratch[pl.ds(pl.multiple_of(d * plan.rows, 8), plan.rows), :] = received_ref[d].astype(F32)
        return unused

    lax.fori_loop(0, plan.devices, cast, 0, unroll=2)


def scalar_of(plan, scratch, first):
    parts = []
    for c in range(plan.mine):
        row = plan.data + first + 3 * c
        parts.append(
            scratch[plan.rows_of(row), :]
            + scratch[plan.rows_of(row + 1), :]
            + scratch[plan.rows_of(row + 2), :]
        )
    return jnp.concatenate(parts, 0)


def tile_values(plan, scratch, weights2, k):
    halves = []
    for h in range(2):
        halves.append(
            jnp.concatenate(
                [
                    scratch[plan.rows_of(c * plan.tiles + 2 * k + h), :].astype(BF16)
                    for c in range(plan.mine)
                ],
                0,
            )
        )
    return lax.dot_general(
        jnp.concatenate(halves, 1), weights2, (((1,), (1,)), ((), ())),
        preferred_element_type=F32,
    )


def turn_kernel(
    plan, received_ref, rhs_ref, weights_ref, noise_ref, residual_ref, alpha_ref, out_ref, scratch,
    out_scratch,
):
    block = 2 * plan.tile_obs
    unpack(plan, received_ref, scratch)
    alpha = scalar_of(plan, scratch, 0)
    alpha_ref[...] = alpha
    alpha = alpha[:, :block]
    noise = jnp.broadcast_to(noise_ref[...], (plan.columns, block))

    def step(k, totals):
        here = pl.ds(pl.multiple_of(k * block, block), block)
        weights2 = pair_weights(weights_ref, k)
        old = rhs_ref[:, here]
        image = tile_values(plan, scratch, weights2, k) + noise * old
        residual = old - alpha * image
        residual_ref[:, here] = residual
        put_parts(plan, out_scratch, residual.astype(BF16), weights2, k)
        return totals[0] + residual * residual, totals[1] + residual * old

    zero = jnp.zeros((plan.columns, block), F32)
    totals = lax.fori_loop(0, plan.tiles // 2, step, (zero, zero), unroll=UNROLL)
    put_sums(plan, out_scratch, totals)
    write_out(plan, out_scratch, out_ref)


def last_kernel(
    plan, received_ref, rhs_ref, weights_ref, noise_ref, old_residual_ref, alpha_ref, *refs
):
    solution_ref, residual_ref, scratch = refs[-3:]
    block = 2 * plan.tile_obs
    unpack(plan, received_ref, scratch)
    alpha = scalar_of(plan, scratch, 0)[:, :block]
    beta = scalar_of(plan, scratch, 3 * plan.mine)[:, :block]
    first_alpha = alpha_ref[:, :block]
    noise = jnp.broadcast_to(noise_ref[...], (plan.columns, block))

    def step(k, unused):
        here = pl.ds(pl.multiple_of(k * block, block), block)
        rhs = rhs_ref[:, here]
        old = old_residual_ref[:, here]
        direction = old + beta * rhs
        image = tile_values(plan, scratch, pair_weights(weights_ref, k), k) + noise * direction
        solution_ref[:, here] = first_alpha * rhs + alpha * direction
        residual_ref[:, here] = old - alpha * image
        return unused

    lax.fori_loop(0, plan.tiles // 2, step, 0, unroll=UNROLL)


VMEM = pl.BlockSpec(memory_space=pltpu.VMEM)
SMEM = pl.BlockSpec(memory_space=pltpu.SMEM)
ANY = pl.BlockSpec(memory_space=pl.ANY)


def by_columns(rhs, tile_weights, tile_owner, tile_row, axis_a, axis_b, coupling, noise):
    peers = lax.axis_size(PEERS)
    part, lvl = lax.axis_size("part"), lax.axis_size("lvl")
    tiles, tile_obs, nodes = tile_weights.shape
    all_columns, width = rhs.shape
    groups = 2 if all_columns % (2 * peers) == 0 else 1
    columns = all_columns // groups
    a_rows, lvl_here, first_axis = axis_a.shape
    b_rows = nodes // part
    levels = lvl * lvl_here
    node_count = levels * first_axis
    place = jnp.stack([lax.axis_index(PEERS), lax.axis_index("half")]).astype(jnp.int32)
    setup_rows = lvl_here * (a_rows + b_rows) + BLOCK
    start = Plan(peers, columns, tiles, tile_obs, nodes, EXTRA + setup_rows)
    plan = Plan(peers, columns, tiles, tile_obs, nodes, EXTRA)
    grid_width = plan.mine * nodes

    owner = tile_owner[:, 0]
    first = owner // lvl * a_rows + tile_row // lvl_here
    target = (owner % lvl * lvl_here + tile_row % lvl_here) * first_axis + first
    index = jnp.stack([target // BASE, target % BASE]).astype(BF16)
    my_b = lax.dynamic_slice_in_dim(axis_b, lax.axis_index("part") * b_rows, b_rows, 1)
    setup = (
        jnp.transpose(axis_a, (1, 0, 2)).reshape(lvl_here * a_rows, first_axis),
        my_b.reshape(lvl_here * b_rows, nodes),
        jnp.concatenate([index, jnp.zeros((BLOCK - 2, tiles), BF16)], 0),
    )

    def exchange(field):
        return lax.all_to_all(field, PEERS, split_axis=0, concat_axis=0, tiled=True)

    def swap(field):
        return lax.ppermute(field, "half", [(0, 1), (1, 0)])

    def shape(*dims, dtype=F32):
        return jax.ShapeDtypeStruct(dims, dtype)

    def part_of(g, *dims):
        return pl.BlockSpec(dims, lambda i: (g,) + (0,) * (len(dims) - 1), memory_space=pltpu.VMEM)

    noise_column = noise[:, None]
    parts_scratch = [pltpu.VMEM((peers * plan.rows, nodes), F32)]
    grid_scratch = [
        pltpu.VMEM((levels, first_axis, first_axis), BF16),
        pltpu.VMEM((node_count, grid_width), BF16),
        pltpu.VMEM((node_count, grid_width), BF16),
        pltpu.VMEM((levels, first_axis, grid_width), F32),
    ]
    sent_shape = shape(peers, plan.rows, nodes, dtype=BF16)
    residual_shape = shape(columns, width)

    def send(g):
        here = start if g == 0 else plan
        return pl.pallas_call(
            lambda *refs: send_kernel(here, *refs),
            out_shape=shape(peers, here.rows, nodes, dtype=BF16),
            in_specs=[part_of(g, columns, width), VMEM] + [VMEM] * 3 * (g == 0),
            out_specs=VMEM,
            scratch_shapes=[pltpu.VMEM((peers * here.rows, nodes), F32)],
            grid=(1,),
        )(rhs, tile_weights, *(setup if g == 0 else ()))

    def read(received):
        return pl.pallas_call(
            lambda *refs: read_setup(start, part, lvl, a_rows, lvl_here, b_rows, *refs),
            out_shape=(
                shape(levels, first_axis // 2, first_axis, dtype=BF16),
                shape(levels, nodes, nodes, dtype=BF16),
                shape(peers, tiles, dtype=jnp.int32),
                shape(tiles, tiles, dtype=jnp.int32),
            ),
            in_specs=[VMEM],
            out_specs=[VMEM] * 4,
            name="read_setup",
        )(received)

    def collected(here, quantities, received, index):
        return pl.pallas_call(
            lambda *refs: collect_kernel(here, quantities, *refs),
            out_shape=shape(node_count + SCALARS, grid_width, dtype=BF16),
            in_specs=[VMEM] * 2,
            out_specs=VMEM,
            scratch_shapes=[pltpu.VMEM((node_count, grid_width), F32)],
        )(received, index)

    def grid(g, own, other, tables, kept):
        keep = (shape(node_count, grid_width), shape(1, grid_width)) if not kept else ()
        return pl.pallas_call(
            lambda *refs: grid_kernel(plan, not kept, g * columns, *refs),
            out_shape=(sent_shape,) + keep,
            in_specs=[SMEM] * 3 + [VMEM] * (6 + len(kept)),
            out_specs=[VMEM] * (1 + len(keep)),
            scratch_shapes=grid_scratch,
        )(coupling, noise, place, own, other, *tables, *kept)

    def turn(g, received):
        return pl.pallas_call(
            lambda *refs: turn_kernel(plan, *refs),
            out_shape=(residual_shape, shape(columns, nodes), sent_shape),
            in_specs=[VMEM, part_of(g, columns, width), VMEM, part_of(g, columns, 1)],
            out_specs=[VMEM] * 3,
            scratch_shapes=parts_scratch * 2,
            grid=(1,),
        )(received, rhs, tile_weights, noise_column)

    def last(g, received, residual, alpha, outputs):
        return pl.pallas_call(
            lambda *refs: last_kernel(plan, *refs),
            out_shape=(shape(*rhs.shape), shape(*rhs.shape)),
            in_specs=[VMEM, part_of(g, columns, width), VMEM, part_of(g, columns, 1), VMEM, VMEM]
            + [ANY] * len(outputs),
            out_specs=[part_of(g, columns, width)] * 2,
            input_output_aliases={6 + i: i for i in range(len(outputs))},
            scratch_shapes=parts_scratch,
            grid=(1,),
        )(received, rhs, tile_weights, noise_column, residual, alpha, *outputs)

    each = range(groups)
    received = [exchange(send(g)) for g in each]
    own_a, full_b, index, index_t = read(received[0])
    other_a = swap(own_a)
    tables = (own_a, other_a, full_b, index_t)
    own = [collected(start if g == 0 else plan, 1, received[g], index) for g in each]
    other = [swap(own[g]) for g in each]
    grids = [grid(g, own[g], other[g], tables, ()) for g in each]
    received = [exchange(grids[g][0]) for g in each]
    turned = [turn(g, received[g]) for g in each]
    received = [exchange(turned[g][2]) for g in each]
    own = [collected(plan, 2, received[g], index) for g in each]
    other = [swap(own[g]) for g in each]
    sent = [grid(g, own[g], other[g], tables, grids[g][1:])[0] for g in each]
    received = [exchange(sent[g]) for g in each]
    outputs = ()
    for g in each:
        outputs = last(g, received[g], turned[g][0], turned[g][1], outputs)
    return outputs


def solution(mesh):
    obs, lvl = mesh.shape["obs"], mesh.shape["lvl"]
    split = Mesh(mesh.devices.reshape(2, obs // 2, lvl), SPLIT)
    in_specs = (
        P(None, SPLIT),
        P(SPLIT, None, None),
        P(SPLIT, None),
        P(SPLIT),
        P(("half", "part"), "lvl", None),
        P("lvl", None, None),
        P(),
        P(),
    )
    out_specs = (P(None, SPLIT), P(None, SPLIT))
    return jax.shard_map(
        by_columns, mesh=split, in_specs=in_specs, out_specs=out_specs, check_vma=False
    )
```

time: 789 us -> 291 us (0.37)
  blocking collectives: 429 us -> 0 us
  local copies, waits for them, and re-layouts: 130 us -> 13.9 us
  Pallas kernels: 0 us -> 93.3 us
  matrix products: 32.4 us -> 0 us
  starting transfers between devices: 18.3 us -> 47.4 us
  other arithmetic: 22.9 us -> 1.94 us
  between operations: 14.5 us -> 0.78 us
    all_to_all x2 -> x0, blocking collectives: 197 us -> none  [the longest x1 98.8 us: on_device(): lax.all_to_all(outgoing, ('obs', 'lvl'), split_axis=0, concat_axis=0, til...]
    psum x3 -> x0, blocking collectives: 118 us -> none  [the longest x2 79.1 us: squared_norm(): return lax.psum(jnp.sum(field * field, axis=1), ('obs', 'lvl'))]
    all_gather x1 -> x0, blocking collectives: 113 us -> none  [on_device(): whole_kernel = lax.all_gather(axis_a, 'obs', axis=0, tiled=True)]
    ppermute x0 -> x5, waiting for transfers between devices: none -> 101 us  [swap(): return lax.ppermute(field, 'half', [(0, 1), (1, 0)])]
    pallas_call x0 -> x15, Pallas kernels: none -> 93.3 us  [the longest x2 29.5 us: turn(): pl.pallas_call(lambda *refs: turn_kernel(plan, *refs), out_shape=(residua...]
    all_to_all x3 -> x8, waiting for transfers between devices: 93.5 us -> 31.6 us  [exchange(): return lax.all_to_all(field, PEERS, split_axis=0, concat_axis=0, tiled=True)]
    all_gather x2 -> x0, waiting for transfers between devices: 43.5 us -> none  [on_device(): lax.all_gather(local_axes(grid), 'lvl', axis=1, tiled=True)]
    gather x4 -> x0, local copies, waits for them, and re-layouts: 38.7 us -> none  [the longest x2 29.3 us: on_device(): grid_values[col_rows].reshape(devices, lvl_cap, col_width, node_cols)]
  transfers between devices with their start and end apart: 5 -> 13, of which waited for: 3 -> 8; matrix products, arithmetic and copies ran while one was open for 4% -> 0% of each run, Pallas kernels for 0% -> 28%
where the time goes in v1:
time: 291 us; the launch traced here: 290 us
  waiting for transfers between devices  133 us (46%)
  Pallas kernels  93.3 us (32%)
  starting transfers between devices  47.4 us (16%)
  local copies, waits for them, and re-layouts  13.9 us (5%)
    ppermute x5, waiting for transfers between devices, swap(): return lax.ppermute(field, 'half', [(0, 1), (1, 0)])  101 us
    all_to_all x8, starting transfers between devices, exchange(): return lax.all_to_all(field, PEERS, split_axis=0, concat_axis=0, tiled=True)  34.5 us
    all_to_all x8, waiting for transfers between devices, exchange(): return lax.all_to_all(field, PEERS, split_axis=0, concat_axis=0, tiled=True)  31.6 us
    pallas_call x2, Pallas kernels, turn(): pl.pallas_call(lambda *refs: turn_kernel(plan, *refs), out_shape=(residua...  29.5 us
    pallas_call x4, Pallas kernels, grid(): pl.pallas_call(lambda *refs: grid_kernel(plan, not kept, g * columns, *re...  19.6 us
    pallas_call x4, Pallas kernels, collected(): pl.pallas_call(lambda *refs: collect_kernel(here, quantities, *refs), out...  18.8 us
    ppermute x5, starting transfers between devices, swap(): return lax.ppermute(field, 'half', [(0, 1), (1, 0)])  12.9 us
    pallas_call x2, Pallas kernels, last(): pl.pallas_call(lambda *refs: last_kernel(plan, *refs), out_shape=(shape(*...  12.7 us
  transfers between devices with their start and end apart: 13, of which 8 were waited for; matrix products, arithmetic and copies ran while one was open for 0% of the time, Pallas kernels for 28%

profile of v1, /device:TPU:0, one launch (start us, length us, event | category | flops | bytes accessed | tf_op | source)
XLA Modules:
  0.0 289.9 jit_solution(8022059815474450022)
XLA Ops:
  0.7 0.7 convert_bitcast_fusion
  1.4 1.3 copy.12
  3.9 5.7 %shard_map.96 = bf16[16,384,128]{2,1,0:T(8,128)(2,1)} custom-call(f32[64,8192]{1,0:T(8,128)} %refs_1_.19, bf16[128,64,128]{2,1,0:T(8,128)(2,1)} %refs_2_.7, bf16[32,128]{1,0:T(8,128)(2,1)} %bitcast.25, bf16[64,128]{1,0:T(8,128)(2,1)} %bitcast.24, bf16[16,128]{1,0:T(8,128)(2,1)} %fusion.2.refs_4_), custom_call_target="tpu_custom_call" | custom-call | tf_op jit(solution)/shard_map/pallas_call | solution.py:422
  9.6 6.3 %all-to-all-start.1 = ((bf16[16,384,128]{2,1,0:T(8,128)(2,1)}), bf16[16,384,128]{2,1,0:T(8,128)(2,1)S(1)}, u32[]{:S(2)}, u32[]{:S(2)}) async-start(bf16[16,384,128]{2,1,0:T(8,128)(2,1)} %shard_map.96), calls=%async_computation.1 | async-start | bytes 3145728 | tf_op jit(solution)/shard_map/all_to_all | solution.py:398
  15.9 4.9 %shard_map.95 = bf16[16,272,128]{2,1,0:T(8,128)(2,1)} custom-call(f32[64,8192]{1,0:T(8,128)} %refs_1_.19, bf16[128,64,128]{2,1,0:T(8,128)(2,1)} %refs_2_.7), custom_call_target="tpu_custom_call" | custom-call | tf_op jit(solution)/shard_map/pallas_call | solution.py:422
  20.8 17.6 %all-to-all-done.1.refs_0_ = bf16[16,384,128]{2,1,0:T(8,128)(2,1)S(1)} async-done(((bf16[16,384,128]{2,1,0:T(8,128)(2,1)}), bf16[16,384,128]{2,1,0:T(8,128)(2,1)S(1)}, u32[]{:S(2)}, u32[]{:S(2)}) %all-to-all-start.1) | async-done | bytes 1572896 | tf_op jit(solution)/shard_map/all_to_all | solution.py:398
  38.4 1.1 copy-done.1
  39.5 3.9 %all-to-all-start = ((bf16[16,272,128]{2,1,0:T(8,128)(2,1)}), bf16[16,272,128]{2,1,0:T(8,128)(2,1)S(1)}, u32[]{:S(2)}, u32[]{:S(2)}) async-start(bf16[16,272,128]{2,1,0:T(8,128)(2,1)} %shard_map.95), calls=%async_computation | async-start | bytes 2228224 | tf_op jit(solution)/shard_map/all_to_all | solution.py:398
  43.5 2.2 read_setup.1
  45.7 4.8 %shard_map.102.refs_3_ = bf16[1032,256]{1,0:T(8,128)(2,1)} custom-call(bf16[16,384,128]{2,1,0:T(8,128)(2,1)} %copy-done.1, s32[16,128]{1,0:T(8,128)} %get-tuple-element.20.refs_1_), custom_call_target="tpu_custom_call" | custom-call | tf_op jit(solution)/shard_map/pallas_call | solution.py:446
  50.5 2.6 collective-permute-start.3
  54.1 28.9 %collective-permute-done.1.refs_6_ = bf16[8,64,128]{2,1,0:T(8,128)(2,1)S(1)} collective-permute-done((bf16[8,64,128]{2,1,0:T(8,128)(2,1)S(1)}, bf16[8,64,128]{2,1,0:T(8,128)(2,1)S(1)}, u32[]{:S(2)}, u32[]{:S(2)}) %collective-permute-start.1) | collective-permute-done | bytes 131104 | tf_op jit(solution)/shard_map/ppermute | solution.py:401
  83.8 4.7 %shard_map.103 = (bf16[16,272,128]{2,1,0:T(8,128)(2,1)}, f32[1024,256]{1,0:T(8,128)}, f32[1,256]{1,0:T(1,128)}) custom-call(f32[8,8]{1,0:T(8,128)} %refs_0_.11, f32[64]{0:T(128)} %refs_1_.17, s32[2]{0:T(128)} %pad_add_fusion.refs_2_, bf16[1032,256]{1,0:T(8,128)(2,1)} %shard_map.102.refs_3_, bf16[1032,256]{1,0:T(8,128)(2,1)} %copy-done.11, ...), custom_call_target="tpu_custom_call" | custom-call | tf_op jit(solution)/shard_map/pallas_call | solution.py:456
  88.5 1.0 copy-done.2
  89.5 4.0 %all-to-all-start.5 = ((bf16[16,272,128]{2,1,0:T(8,128)(2,1)}), bf16[16,272,128]{2,1,0:T(8,128)(2,1)S(1)}, u32[]{:S(2)}, u32[]{:S(2)}) async-start(bf16[16,272,128]{2,1,0:T(8,128)(2,1)} %get-tuple-element.30), calls=%async_computation.5 | async-start | bytes 2228224 | tf_op jit(solution)/shard_map/all_to_all | solution.py:398
  93.5 4.6 %shard_map.97.refs_3_ = bf16[1032,256]{1,0:T(8,128)(2,1)} custom-call(bf16[16,272,128]{2,1,0:T(8,128)(2,1)} %copy-done.2, s32[16,128]{1,0:T(8,128)} %get-tuple-element.20.refs_1_), custom_call_target="tpu_custom_call" | custom-call | tf_op jit(solution)/shard_map/pallas_call | solution.py:446
  98.2 3.4 %collective-permute-start = (bf16[1032,256]{1,0:T(8,128)(2,1)}, bf16[1032,256]{1,0:T(8,128)(2,1)S(1)}, u32[]{:S(2)}, u32[]{:S(2)}) collective-permute-start(bf16[1032,256]{1,0:T(8,128)(2,1)} %shard_map.97.refs_3_), channel_id=1, source_target_pairs={{0,16},{16,0},{1,17},{17,1},{2,18},{18,2},{3,19},{19,3},{4,20},{20... | collective-permute-start | bytes 1585160 | tf_op jit(solution)/shard_map/ppermute | solution.py:401
  101.5 24.2 %collective-permute-done.refs_4_ = bf16[1032,256]{1,0:T(8,128)(2,1)S(1)} collective-permute-done((bf16[1032,256]{1,0:T(8,128)(2,1)}, bf16[1032,256]{1,0:T(8,128)(2,1)S(1)}, u32[]{:S(2)}, u32[]{:S(2)}) %collective-permute-start) | collective-permute-done | bytes 528416 | tf_op jit(solution)/shard_map/ppermute | solution.py:401
  125.7 0.8 copy-done.13
  126.5 4.7 %shard_map.98 = (bf16[16,272,128]{2,1,0:T(8,128)(2,1)}, f32[1024,256]{1,0:T(8,128)}, f32[1,256]{1,0:T(1,128)}) custom-call(f32[8,8]{1,0:T(8,128)} %refs_0_.11, f32[64]{0:T(128)} %refs_1_.17, s32[2]{0:T(128)} %pad_add_fusion.refs_2_, bf16[1032,256]{1,0:T(8,128)(2,1)} %shard_map.97.refs_3_, bf16[1032,256]{1,0:T(8,128)(2,1)} %copy-done.13, ...), custom_call_target="tpu_custom_call" | custom-call | tf_op jit(solution)/shard_map/pallas_call | solution.py:456
  131.2 1.0 copy-done.4
  132.2 4.2 %all-to-all-start.2 = ((bf16[16,272,128]{2,1,0:T(8,128)(2,1)}), bf16[16,272,128]{2,1,0:T(8,128)(2,1)S(1)}, u32[]{:S(2)}, u32[]{:S(2)}) async-start(bf16[16,272,128]{2,1,0:T(8,128)(2,1)} %get-tuple-element.24), calls=%async_computation.2 | async-start | bytes 2228224 | tf_op jit(solution)/shard_map/all_to_all | solution.py:398
  137.1 14.7 %shard_map.104 = (f32[32,8192]{1,0:T(8,128)}, f32[32,128]{1,0:T(8,128)}, bf16[16,272,128]{2,1,0:T(8,128)(2,1)}) custom-call(bf16[16,272,128]{2,1,0:T(8,128)(2,1)} %copy-done.4, f32[64,8192]{1,0:T(8,128)} %refs_1_.19, bf16[128,64,128]{2,1,0:T(8,128)(2,1)} %refs_2_.7, f32[64,1]{1,0:T(8,128)} %copy.13.refs_3_), custom_call_target="tpu_custom_call" | custom-call | tf_op jit(solution)/shard_map/pallas_call | solution.py:465
  151.8 1.4 all-to-all-done.2.refs_0_
  153.2 1.0 copy-done.6
  154.2 3.7 %all-to-all-start.6 = ((bf16[16,272,128]{2,1,0:T(8,128)(2,1)}), bf16[16,272,128]{2,1,0:T(8,128)(2,1)S(1)}, u32[]{:S(2)}, u32[]{:S(2)}) async-start(bf16[16,272,128]{2,1,0:T(8,128)(2,1)} %get-tuple-element.31), calls=%async_computation.6 | async-start | bytes 2228224 | tf_op jit(solution)/shard_map/all_to_all | solution.py:398
  158.0 14.7 %shard_map.99 = (f32[32,8192]{1,0:T(8,128)}, f32[32,128]{1,0:T(8,128)}, bf16[16,272,128]{2,1,0:T(8,128)(2,1)}) custom-call(bf16[16,272,128]{2,1,0:T(8,128)(2,1)} %copy-done.6, f32[64,8192]{1,0:T(8,128)} %refs_1_.19, bf16[128,64,128]{2,1,0:T(8,128)(2,1)} %refs_2_.7, f32[64,1]{1,0:T(8,128)} %copy.13.refs_3_), custom_call_target="tpu_custom_call" | custom-call | tf_op jit(solution)/shard_map/pallas_call | solution.py:465
  172.7 2.1 all-to-all-done.6.refs_0_
  174.8 1.0 copy-done.7
  175.8 3.9 %all-to-all-start.3 = ((bf16[16,272,128]{2,1,0:T(8,128)(2,1)}), bf16[16,272,128]{2,1,0:T(8,128)(2,1)S(1)}, u32[]{:S(2)}, u32[]{:S(2)}) async-start(bf16[16,272,128]{2,1,0:T(8,128)(2,1)} %get-tuple-element.25), calls=%async_computation.3 | async-start | bytes 2228224 | tf_op jit(solution)/shard_map/all_to_all | solution.py:398
  179.7 4.7 %shard_map.105.refs_3_ = bf16[1032,256]{1,0:T(8,128)(2,1)} custom-call(bf16[16,272,128]{2,1,0:T(8,128)(2,1)} %copy-done.7, s32[16,128]{1,0:T(8,128)} %get-tuple-element.20.refs_1_), custom_call_target="tpu_custom_call" | custom-call | tf_op jit(solution)/shard_map/pallas_call | solution.py:446
  184.3 3.3 %collective-permute-start.4 = (bf16[1032,256]{1,0:T(8,128)(2,1)}, bf16[1032,256]{1,0:T(8,128)(2,1)S(1)}, u32[]{:S(2)}, u32[]{:S(2)}) collective-permute-start(bf16[1032,256]{1,0:T(8,128)(2,1)} %shard_map.105.refs_3_), channel_id=1, source_target_pairs={{0,16},{16,0},{1,17},{17,1},{2,18},{18,2},{3,19},{19,3},{4,20},{20... | collective-permute-start | bytes 1585160 | tf_op jit(solution)/shard_map/ppermute | solution.py:401
  187.6 23.8 %collective-permute-done.4.refs_4_ = bf16[1032,256]{1,0:T(8,128)(2,1)S(1)} collective-permute-done((bf16[1032,256]{1,0:T(8,128)(2,1)}, bf16[1032,256]{1,0:T(8,128)(2,1)S(1)}, u32[]{:S(2)}, u32[]{:S(2)}) %collective-permute-start.4) | collective-permute-done | bytes 528416 | tf_op jit(solution)/shard_map/ppermute | solution.py:401
  211.4 0.8 copy-done.14
  212.2 5.1 %shard_map.106 = bf16[16,272,128]{2,1,0:T(8,128)(2,1)} custom-call(f32[8,8]{1,0:T(8,128)} %refs_0_.11, f32[64]{0:T(128)} %refs_1_.17, s32[2]{0:T(128)} %pad_add_fusion.refs_2_, bf16[1032,256]{1,0:T(8,128)(2,1)} %shard_map.105.refs_3_, bf16[1032,256]{1,0:T(8,128)(2,1)} %copy-done.14, bf16[8,64,128]{2,1,0:T(8,128)(2,1)} %get-tuple-element.21.refs_5_, ...), custom_call_target="tpu_custom_call" | custom-call | tf_op jit(solution)/shard_map/pallas_call | solution.py:456
  217.3 1.0 copy-done.5
  218.3 4.3 %all-to-all-start.7 = ((bf16[16,272,128]{2,1,0:T(8,128)(2,1)}), bf16[16,272,128]{2,1,0:T(8,128)(2,1)S(1)}, u32[]{:S(2)}, u32[]{:S(2)}) async-start(bf16[16,272,128]{2,1,0:T(8,128)(2,1)} %shard_map.106), calls=%async_computation.7 | async-start | bytes 2228224 | tf_op jit(solution)/shard_map/all_to_all | solution.py:398
  222.6 4.6 %shard_map.100.refs_3_ = bf16[1032,256]{1,0:T(8,128)(2,1)} custom-call(bf16[16,272,128]{2,1,0:T(8,128)(2,1)} %copy-done.5, s32[16,128]{1,0:T(8,128)} %get-tuple-element.20.refs_1_), custom_call_target="tpu_custom_call" | custom-call | tf_op jit(solution)/shard_map/pallas_call | solution.py:446
  227.2 3.3 %collective-permute-start.2 = (bf16[1032,256]{1,0:T(8,128)(2,1)}, bf16[1032,256]{1,0:T(8,128)(2,1)S(1)}, u32[]{:S(2)}, u32[]{:S(2)}) collective-permute-start(bf16[1032,256]{1,0:T(8,128)(2,1)} %shard_map.100.refs_3_), channel_id=1, source_target_pairs={{0,16},{16,0},{1,17},{17,1},{2,18},{18,2},{3,19},{19,3},{4,20},{20... | collective-permute-start | bytes 1585160 | tf_op jit(solution)/shard_map/ppermute | solution.py:401
  230.5 24.2 %collective-permute-done.2.refs_4_ = bf16[1032,256]{1,0:T(8,128)(2,1)S(1)} collective-permute-done((bf16[1032,256]{1,0:T(8,128)(2,1)}, bf16[1032,256]{1,0:T(8,128)(2,1)S(1)}, u32[]{:S(2)}, u32[]{:S(2)}) %collective-permute-start.2) | collective-permute-done | bytes 528416 | tf_op jit(solution)/shard_map/ppermute | solution.py:401
  254.6 0.8 copy-done.12
  255.4 5.1 %shard_map.101 = bf16[16,272,128]{2,1,0:T(8,128)(2,1)} custom-call(f32[8,8]{1,0:T(8,128)} %refs_0_.11, f32[64]{0:T(128)} %refs_1_.17, s32[2]{0:T(128)} %pad_add_fusion.refs_2_, bf16[1032,256]{1,0:T(8,128)(2,1)} %shard_map.100.refs_3_, bf16[1032,256]{1,0:T(8,128)(2,1)} %copy-done.12, bf16[8,64,128]{2,1,0:T(8,128)(2,1)} %get-tuple-element.21.refs_5_, ...), custom_call_target="tpu_custom_call" | custom-call | tf_op jit(solution)/shard_map/pallas_call | solution.py:456
  260.6 1.0 copy-done.3
  261.5 4.2 %all-to-all-start.4 = ((bf16[16,272,128]{2,1,0:T(8,128)(2,1)}), bf16[16,272,128]{2,1,0:T(8,128)(2,1)S(1)}, u32[]{:S(2)}, u32[]{:S(2)}) async-start(bf16[16,272,128]{2,1,0:T(8,128)(2,1)} %shard_map.101), calls=%async_computation.4 | async-start | bytes 2228224 | tf_op jit(solution)/shard_map/all_to_all | solution.py:398
  265.7 6.3 %shard_map.107 = (f32[64,8192]{1,0:T(8,128)}, f32[64,8192]{1,0:T(8,128)}) custom-call(bf16[16,272,128]{2,1,0:T(8,128)(2,1)} %copy-done.3, f32[64,8192]{1,0:T(8,128)} %refs_1_.19, bf16[128,64,128]{2,1,0:T(8,128)(2,1)} %refs_2_.7, f32[64,1]{1,0:T(8,128)} %copy.13.refs_3_, f32[32,8192]{1,0:T(8,128)} %get-tuple-element.34.refs_4_, ...), custom_call_target="tpu_custom_call" | custom-call | tf_op jit(solution)/shard_map/pallas_call | solution.py:475
  272.1 10.5 %all-to-all-done.4.refs_0_ = bf16[16,272,128]{2,1,0:T(8,128)(2,1)S(1)} async-done(((bf16[16,272,128]{2,1,0:T(8,128)(2,1)}), bf16[16,272,128]{2,1,0:T(8,128)(2,1)S(1)}, u32[]{:S(2)}, u32[]{:S(2)}) %all-to-all-start.4) | async-done | bytes 1114144 | tf_op jit(solution)/shard_map/all_to_all | solution.py:398
  282.6 1.0 copy-done.8
  283.6 6.3 %shard_map.108 = (f32[64,8192]{1,0:T(8,128)}, f32[64,8192]{1,0:T(8,128)}) custom-call(bf16[16,272,128]{2,1,0:T(8,128)(2,1)} %copy-done.8, f32[64,8192]{1,0:T(8,128)} %refs_1_.19, bf16[128,64,128]{2,1,0:T(8,128)(2,1)} %refs_2_.7, f32[64,1]{1,0:T(8,128)} %copy.13.refs_3_, ...), custom_call_target="tpu_custom_call", output_to_operand_aliasing={{0}: (6, {}), {1}: (7, {})} | custom-call | tf_op jit(solution)/shard_map/pallas_call | solution.py:475
  (32 shorter events, 3.7 us)
Async XLA Ops:
  0.6 2.7 copy-start
  9.6 28.8 %all-to-all-start.1 = ((bf16[16,384,128]{2,1,0:T(8,128)(2,1)}), bf16[16,384,128]{2,1,0:T(8,128)(2,1)S(1)}, u32[]{:S(2)}, u32[]{:S(2)}) async-start(bf16[16,384,128]{2,1,0:T(8,128)(2,1)} %shard_map.96), calls=%async_computation.1 | async-start | bytes 3145728 | tf_op jit(solution)/shard_map/all_to_all | solution.py:398
  38.4 1.1 copy-start.1
  39.5 49.0 %all-to-all-start = ((bf16[16,272,128]{2,1,0:T(8,128)(2,1)}), bf16[16,272,128]{2,1,0:T(8,128)(2,1)S(1)}, u32[]{:S(2)}, u32[]{:S(2)}) async-start(bf16[16,272,128]{2,1,0:T(8,128)(2,1)} %shard_map.95), calls=%async_computation | async-start | bytes 2228224 | tf_op jit(solution)/shard_map/all_to_all | solution.py:398
  45.7 7.4 %copy-start.9 = (bf16[8,64,128]{2,1,0:T(8,128)(2,1)S(1)}, bf16[8,64,128]{2,1,0:T(8,128)(2,1)}, u32[]{:S(2)}) copy-start(bf16[8,64,128]{2,1,0:T(8,128)(2,1)} %get-tuple-element.21.refs_5_) | copy-start | bytes 393220
  50.5 32.4 %collective-permute-start.3 = (bf16[1032,256]{1,0:T(8,128)(2,1)}, bf16[1032,256]{1,0:T(8,128)(2,1)S(1)}, u32[]{:S(2)}, u32[]{:S(2)}) collective-permute-start(bf16[1032,256]{1,0:T(8,128)(2,1)} %shard_map.102.refs_3_), channel_id=1, source_target_pairs={{0,16},{16,0},{1,17},{17,1},{2,18},{18,2},{3,19},{19,3},{4,20},{20... | collective-permute-start | bytes 1585160 | tf_op jit(solution)/shard_map/ppermute | solution.py:401
  53.1 29.8 %collective-permute-start.1 = (bf16[8,64,128]{2,1,0:T(8,128)(2,1)S(1)}, bf16[8,64,128]{2,1,0:T(8,128)(2,1)S(1)}, u32[]{:S(2)}, u32[]{:S(2)}) collective-permute-start(bf16[8,64,128]{2,1,0:T(8,128)(2,1)S(1)} %copy-done.9), channel_id=1, source_target_pairs={{0,16},{16,0},{1,17},{17,1},{2,18},{18,2},{3,19},{19,3},{4,20},{20... | collective-permute-start | bytes 393224 | tf_op jit(solution)/shard_map/ppermute | solution.py:401
  82.9 0.7 copy-start.10
  82.9 0.8 copy-start.11
  88.5 1.0 copy-start.2
  89.5 41.7 %all-to-all-start.5 = ((bf16[16,272,128]{2,1,0:T(8,128)(2,1)}), bf16[16,272,128]{2,1,0:T(8,128)(2,1)S(1)}, u32[]{:S(2)}, u32[]{:S(2)}) async-start(bf16[16,272,128]{2,1,0:T(8,128)(2,1)} %get-tuple-element.30), calls=%async_computation.5 | async-start | bytes 2228224 | tf_op jit(solution)/shard_map/all_to_all | solution.py:398
  98.2 27.5 %collective-permute-start = (bf16[1032,256]{1,0:T(8,128)(2,1)}, bf16[1032,256]{1,0:T(8,128)(2,1)S(1)}, u32[]{:S(2)}, u32[]{:S(2)}) collective-permute-start(bf16[1032,256]{1,0:T(8,128)(2,1)} %shard_map.97.refs_3_), channel_id=1, source_target_pairs={{0,16},{16,0},{1,17},{17,1},{2,18},{18,2},{3,19},{19,3},{4,20},{20... | collective-permute-start | bytes 1585160 | tf_op jit(solution)/shard_map/ppermute | solution.py:401
  125.7 0.8 copy-start.13
  131.2 1.0 copy-start.4
  131.2 5.2 %copy-start.15 = (f32[64]{0:T(128)S(1)}, f32[64]{0:T(128)}, u32[]{:S(2)}) copy-start(f32[64]{0:T(128)} %refs_1_.17) | copy-start | bytes 772
  132.2 21.0 %all-to-all-start.2 = ((bf16[16,272,128]{2,1,0:T(8,128)(2,1)}), bf16[16,272,128]{2,1,0:T(8,128)(2,1)S(1)}, u32[]{:S(2)}, u32[]{:S(2)}) async-start(bf16[16,272,128]{2,1,0:T(8,128)(2,1)} %get-tuple-element.24), calls=%async_computation.2 | async-start | bytes 2228224 | tf_op jit(solution)/shard_map/all_to_all | solution.py:398
  153.2 1.0 copy-start.6
  154.2 20.6 %all-to-all-start.6 = ((bf16[16,272,128]{2,1,0:T(8,128)(2,1)}), bf16[16,272,128]{2,1,0:T(8,128)(2,1)S(1)}, u32[]{:S(2)}, u32[]{:S(2)}) async-start(bf16[16,272,128]{2,1,0:T(8,128)(2,1)} %get-tuple-element.31), calls=%async_computation.6 | async-start | bytes 2228224 | tf_op jit(solution)/shard_map/all_to_all | solution.py:398
  174.8 1.0 copy-start.7
  175.8 41.5 %all-to-all-start.3 = ((bf16[16,272,128]{2,1,0:T(8,128)(2,1)}), bf16[16,272,128]{2,1,0:T(8,128)(2,1)S(1)}, u32[]{:S(2)}, u32[]{:S(2)}) async-start(bf16[16,272,128]{2,1,0:T(8,128)(2,1)} %get-tuple-element.25), calls=%async_computation.3 | async-start | bytes 2228224 | tf_op jit(solution)/shard_map/all_to_all | solution.py:398
  184.3 27.1 %collective-permute-start.4 = (bf16[1032,256]{1,0:T(8,128)(2,1)}, bf16[1032,256]{1,0:T(8,128)(2,1)S(1)}, u32[]{:S(2)}, u32[]{:S(2)}) collective-permute-start(bf16[1032,256]{1,0:T(8,128)(2,1)} %shard_map.105.refs_3_), channel_id=1, source_target_pairs={{0,16},{16,0},{1,17},{17,1},{2,18},{18,2},{3,19},{19,3},{4,20},{20... | collective-permute-start | bytes 1585160 | tf_op jit(solution)/shard_map/ppermute | solution.py:401
  211.4 0.8 copy-start.14
  217.3 1.0 copy-start.5
  218.3 42.3 %all-to-all-start.7 = ((bf16[16,272,128]{2,1,0:T(8,128)(2,1)}), bf16[16,272,128]{2,1,0:T(8,128)(2,1)S(1)}, u32[]{:S(2)}, u32[]{:S(2)}) async-start(bf16[16,272,128]{2,1,0:T(8,128)(2,1)} %shard_map.106), calls=%async_computation.7 | async-start | bytes 2228224 | tf_op jit(solution)/shard_map/all_to_all | solution.py:398
  227.2 27.4 %collective-permute-start.2 = (bf16[1032,256]{1,0:T(8,128)(2,1)}, bf16[1032,256]{1,0:T(8,128)(2,1)S(1)}, u32[]{:S(2)}, u32[]{:S(2)}) collective-permute-start(bf16[1032,256]{1,0:T(8,128)(2,1)} %shard_map.100.refs_3_), channel_id=1, source_target_pairs={{0,16},{16,0},{1,17},{17,1},{2,18},{18,2},{3,19},{19,3},{4,20},{20... | collective-permute-start | bytes 1585160 | tf_op jit(solution)/shard_map/ppermute | solution.py:401
  254.6 0.8 copy-start.12
  260.5 1.0 copy-start.3
  261.5 21.0 %all-to-all-start.4 = ((bf16[16,272,128]{2,1,0:T(8,128)(2,1)}), bf16[16,272,128]{2,1,0:T(8,128)(2,1)S(1)}, u32[]{:S(2)}, u32[]{:S(2)}) async-start(bf16[16,272,128]{2,1,0:T(8,128)(2,1)} %shard_map.101), calls=%async_computation.4 | async-start | bytes 2228224 | tf_op jit(solution)/shard_map/all_to_all | solution.py:398
  282.6 1.0 copy-start.8

commit v2 on v1

--- a/solution.py
+++ b/solution.py
@@ -15,6 +15,7 @@
 BLOCK = 16
 SCALARS = 8
 UNROLL = 8
+VMEM_LIMIT = 28 * 1024 * 1024
 BASE = 128
 
 
@@ -194,31 +195,30 @@
             out_ref[j * group + h, plan.data : plan.data + EXTRA] = extra
 
 
-def read_setup(
-    plan, part, lvl, a_rows, lvl_here, b_rows, received_ref, axis_a_ref, axis_b_ref, index_ref,
-    index_t_ref,
-):
-    base = plan.data + EXTRA
-    for o in range(part):
-        for v in range(lvl):
-            for l in range(lvl_here):
-                row = base + l * a_rows
-                axis_a_ref[v * lvl_here + l, o * a_rows : (o + 1) * a_rows] = received_ref[
-                    o * lvl + v, row : row + a_rows
-                ]
-                row = base + lvl_here * a_rows + l * b_rows
-                axis_b_ref[v * lvl_here + l, o * b_rows : (o + 1) * b_rows] = received_ref[
-                    o * lvl + v, row : row + b_rows
-                ]
-    row = base + lvl_here * (a_rows + b_rows)
+def read_index(plan, base, received_ref, index_ref, index_t_ref):
     for d in range(plan.devices):
-        split = received_ref[d, row : row + 8].astype(F32)
+        split = received_ref[d, base : base + 8].astype(F32)
         index_ref[d : d + 1] = (split[0:1] * float(BASE) + split[1:2]).astype(jnp.int32)
     square = index_ref[...].astype(F32)
     square = jnp.concatenate(
         [square] + [jnp.zeros((plan.tiles - plan.devices, plan.tiles), F32)], 0
     )
     index_t_ref[...] = square.T.astype(jnp.int32)
+
+
+def read_axes(plan, base, lvl, received_ref, own_a_ref, other_a_ref):
+    part = plan.devices // lvl
+    lvl_here = own_a_ref.shape[0] // lvl
+    for o in range(part):
+        for v in range(lvl):
+            row = base
+            for table_ref in (own_a_ref, other_a_ref):
+                count = table_ref.shape[1] // part
+                for l in range(lvl_here):
+                    table_ref[v * lvl_here + l, o * count : (o + 1) * count] = received_ref[
+                        o * lvl + v, row : row + count
+                    ]
+                    row += count
 
 
 def collect_kernel(plan, quantities, received_ref, index_ref, out_ref, acc_ref):
@@ -234,10 +234,15 @@
 
 
 def grid_kernel(
-    plan, opening, start_column, coupling_ref, noise_ref, place_ref, own_ref, other_ref, own_a_ref,
-    other_a_ref, axis_b_ref, index_t_ref, *refs,
+    plan, opening, lvl, start_column, coupling_ref, noise_ref, place_ref, own_ref, other_ref,
+    own_a_ref, other_a_ref, index_t_ref, *refs,
 ):
-    axis_a_ref, sums_ref, grid_ref, spread_ref = refs[-4:]
+    axis_a_ref, axis_b_ref, sums_ref, grid_ref, spread_ref = refs[-5:]
+    b_refs, refs = refs[:lvl], refs[lvl:]
+    lvl_here = axis_b_ref.shape[0] // lvl
+    for k in range(lvl):
+        source = (place_ref[2] + lvl - k) % lvl
+        axis_b_ref[pl.ds(source * lvl_here, lvl_here)] = b_refs[k][...]
     node_count, _ = sums_ref.shape
     half = own_a_ref.shape[1]
     axis_a_ref[:, pl.ds(pl.multiple_of(place_ref[1] * half, half), half)] = own_a_ref[...]
@@ -364,22 +369,22 @@
 VMEM = pl.BlockSpec(memory_space=pltpu.VMEM)
 SMEM = pl.BlockSpec(memory_space=pltpu.SMEM)
 ANY = pl.BlockSpec(memory_space=pl.ANY)
+PARAMS = pltpu.CompilerParams(vmem_limit_bytes=VMEM_LIMIT)
 
 
 def by_columns(rhs, tile_weights, tile_owner, tile_row, axis_a, axis_b, coupling, noise):
     peers = lax.axis_size(PEERS)
-    part, lvl = lax.axis_size("part"), lax.axis_size("lvl")
+    lvl = lax.axis_size("lvl")
     tiles, tile_obs, nodes = tile_weights.shape
     all_columns, width = rhs.shape
     groups = 2 if all_columns % (2 * peers) == 0 else 1
     columns = all_columns // groups
     a_rows, lvl_here, first_axis = axis_a.shape
-    b_rows = nodes // part
     levels = lvl * lvl_here
     node_count = levels * first_axis
-    place = jnp.stack([lax.axis_index(PEERS), lax.axis_index("half")]).astype(jnp.int32)
-    setup_rows = lvl_here * (a_rows + b_rows) + BLOCK
-    start = Plan(peers, columns, tiles, tile_obs, nodes, EXTRA + setup_rows)
+    place = jnp.stack(
+        [lax.axis_index(PEERS), lax.axis_index("half"), lax.axis_index("lvl")]
+    ).astype(jnp.int32)
     plan = Plan(peers, columns, tiles, tile_obs, nodes, EXTRA)
     grid_width = plan.mine * nodes
 
@@ -387,18 +392,23 @@
     first = owner // lvl * a_rows + tile_row // lvl_here
     target = (owner % lvl * lvl_here + tile_row % lvl_here) * first_axis + first
     index = jnp.stack([target // BASE, target % BASE]).astype(BF16)
-    my_b = lax.dynamic_slice_in_dim(axis_b, lax.axis_index("part") * b_rows, b_rows, 1)
-    setup = (
-        jnp.transpose(axis_a, (1, 0, 2)).reshape(lvl_here * a_rows, first_axis),
-        my_b.reshape(lvl_here * b_rows, nodes),
-        jnp.concatenate([index, jnp.zeros((BLOCK - 2, tiles), BF16)], 0),
-    )
 
     def exchange(field):
         return lax.all_to_all(field, PEERS, split_axis=0, concat_axis=0, tiled=True)
 
     def swap(field):
         return lax.ppermute(field, "half", [(0, 1), (1, 0)])
+
+    my_a = jnp.transpose(axis_a, (1, 0, 2)).reshape(lvl_here * a_rows, first_axis)
+    tables = [my_a, swap(my_a)]
+    setups = [[] for _ in range(groups)]
+    setups[0] += [jnp.concatenate([index, jnp.zeros((BLOCK - 2, tiles), BF16)], 0)]
+    setups[-1] += tables
+    starts = [
+        Plan(peers, columns, tiles, tile_obs, nodes, EXTRA + sum(t.shape[0] for t in setup))
+        for setup in setups
+    ]
+    tables_row = starts[-1].rows - sum(t.shape[0] for t in tables)
 
     def shape(*dims, dtype=F32):
         return jax.ShapeDtypeStruct(dims, dtype)
@@ -410,6 +420,7 @@
     parts_scratch = [pltpu.VMEM((peers * plan.rows, nodes), F32)]
     grid_scratch = [
         pltpu.VMEM((levels, first_axis, first_axis), BF16),
+        pltpu.VMEM((levels, nodes, nodes), BF16),
         pltpu.VMEM((node_count, grid_width), BF16),
         pltpu.VMEM((node_count, grid_width), BF16),
         pltpu.VMEM((levels, first_axis, grid_width), F32),
@@ -418,28 +429,41 @@
     residual_shape = shape(columns, width)
 
     def send(g):
-        here = start if g == 0 else plan
+        here = starts[g]
         return pl.pallas_call(
             lambda *refs: send_kernel(here, *refs),
             out_shape=shape(peers, here.rows, nodes, dtype=BF16),
-            in_specs=[part_of(g, columns, width), VMEM] + [VMEM] * 3 * (g == 0),
+            in_specs=[part_of(g, columns, width), VMEM] + [VMEM] * len(setups[g]),
             out_specs=VMEM,
             scratch_shapes=[pltpu.VMEM((peers * here.rows, nodes), F32)],
             grid=(1,),
-        )(rhs, tile_weights, *(setup if g == 0 else ()))
-
-    def read(received):
-        return pl.pallas_call(
-            lambda *refs: read_setup(start, part, lvl, a_rows, lvl_here, b_rows, *refs),
+            compiler_params=PARAMS,
+        )(rhs, tile_weights, *setups[g])
+
+    def find(received):
+        return pl.pallas_call(
+            lambda *refs: read_index(plan, plan.data + EXTRA, *refs),
             out_shape=(
-                shape(levels, first_axis // 2, first_axis, dtype=BF16),
-                shape(levels, nodes, nodes, dtype=BF16),
                 shape(peers, tiles, dtype=jnp.int32),
                 shape(tiles, tiles, dtype=jnp.int32),
             ),
             in_specs=[VMEM],
-            out_specs=[VMEM] * 4,
-            name="read_setup",
+            out_specs=[VMEM] * 2,
+            compiler_params=PARAMS,
+            name="read_index",
+        )(received)
+
+    def read(received):
+        return pl.pallas_call(
+            lambda *refs: read_axes(plan, tables_row, lvl, *refs),
+            out_shape=(
+                shape(levels, first_axis // 2, first_axis, dtype=BF16),
+                shape(levels, first_axis // 2, first_axis, dtype=BF16),
+            ),
+            in_specs=[VMEM],
+            out_specs=[VMEM] * 2,
+            compiler_params=PARAMS,
+            name="read_axes",
         )(received)
 
     def collected(here, quantities, received, index):
@@ -449,16 +473,18 @@
             in_specs=[VMEM] * 2,
             out_specs=VMEM,
             scratch_shapes=[pltpu.VMEM((node_count, grid_width), F32)],
+            compiler_params=PARAMS,
         )(received, index)
 
     def grid(g, own, other, tables, kept):
         keep = (shape(node_count, grid_width), shape(1, grid_width)) if not kept else ()
         return pl.pallas_call(
-            lambda *refs: grid_kernel(plan, not kept, g * columns, *refs),
+            lambda *refs: grid_kernel(plan, not kept, lvl, g * columns, *refs),
             out_shape=(sent_shape,) + keep,
-            in_specs=[SMEM] * 3 + [VMEM] * (6 + len(kept)),
+            in_specs=[SMEM] * 3 + [VMEM] * (2 + len(tables) + len(kept)),
             out_specs=[VMEM] * (1 + len(keep)),
             scratch_shapes=grid_scratch,
+            compiler_params=PARAMS,
         )(coupling, noise, place, own, other, *tables, *kept)
 
     def turn(g, received):
@@ -469,6 +495,7 @@
             out_specs=[VMEM] * 3,
             scratch_shapes=parts_scratch * 2,
             grid=(1,),
+            compiler_params=PARAMS,
         )(received, rhs, tile_weights, noise_column)
 
     def last(g, received, residual, alpha, outputs):
@@ -481,14 +508,19 @@
             input_output_aliases={6 + i: i for i in range(len(outputs))},
             scratch_shapes=parts_scratch,
             grid=(1,),
+            compiler_params=PARAMS,
         )(received, rhs, tile_weights, noise_column, residual, alpha, *outputs)
 
     each = range(groups)
     received = [exchange(send(g)) for g in each]
-    own_a, full_b, index, index_t = read(received[0])
-    other_a = swap(own_a)
-    tables = (own_a, other_a, full_b, index_t)
-    own = [collected(start if g == 0 else plan, 1, received[g], index) for g in each]
+    all_b = [axis_b]
+    for k in range(1, lvl):
+        all_b.append(
+            lax.ppermute(axis_b, "lvl", [(v, (v + k) % lvl) for v in range(lvl)])
+        )
+    index, index_t = find(received[0])
+    tables = (*read(received[-1]), index_t, *all_b)
+    own = [collected(starts[g], 1, received[g], index) for g in each]
     other = [swap(own[g]) for g in each]
     grids = [grid(g, own[g], other[g], tables, ()) for g in each]
     received = [exchange(grids[g][0]) for g in each]

time: 291 us -> 273 us (0.938)
  Pallas kernels: 93.3 us -> 63.1 us
  local copies, waits for them, and re-layouts: 13.9 us -> 32.6 us
  waiting for transfers between devices: 133 us -> 122 us
    unnamed x32 -> x114, local copies, waits for them, and re-layouts: 11.3 us -> 32.5 us
    ppermute x5, waiting for transfers between devices: 101 us -> 90 us  [swap(): return lax.ppermute(field, 'half', [(0, 1), (1, 0)])]
    pallas_call x5 -> x6, Pallas kernels: 21.8 us -> 13.8 us  [the longest x4 13.7 us: grid(): pl.pallas_call(lambda *refs: grid_kernel(plan, not kept, lvl, g * columns...]
    pallas_call x4, Pallas kernels: 18.8 us -> 12.3 us  [collected(): pl.pallas_call(lambda *refs: collect_kernel(here, quantities, *refs), out...]
    pallas_call x2, Pallas kernels: 29.5 us -> 23.5 us  [turn(): pl.pallas_call(lambda *refs: turn_kernel(plan, *refs), out_shape=(residua...]
    pallas_call x2, Pallas kernels: 10.6 us -> 4.62 us  [send(): pl.pallas_call(lambda *refs: send_kernel(here, *refs), out_shape=shape(pe...]
    all_to_all x8, starting transfers between devices: 34.5 us -> 39.9 us  [exchange(): return lax.all_to_all(field, PEERS, split_axis=0, concat_axis=0, tiled=True)]
    ppermute x5, starting transfers between devices: 12.9 us -> 8.13 us  [swap(): return lax.ppermute(field, 'half', [(0, 1), (1, 0)])]
  transfers between devices with their start and end apart: 13 -> 16, of which waited for: 8 -> 9; matrix products, arithmetic and copies ran while one was open for 0% -> 0% of each run, Pallas kernels for 28% -> 19%
where the time goes in v2:
time: 273 us; the launch traced here: 271 us
  waiting for transfers between devices  122 us (45%)
  Pallas kernels  63.1 us (23%)
  starting transfers between devices  50.3 us (18%)
  local copies, waits for them, and re-layouts  32.6 us (12%)
    ppermute x5, waiting for transfers between devices, swap(): return lax.ppermute(field, 'half', [(0, 1), (1, 0)])  90 us
    all_to_all x8, starting transfers between devices, exchange(): return lax.all_to_all(field, PEERS, split_axis=0, concat_axis=0, tiled=True)  39.9 us
    unnamed x114, local copies, waits for them, and re-layouts  32.5 us
    all_to_all x8, waiting for transfers between devices, exchange(): return lax.all_to_all(field, PEERS, split_axis=0, concat_axis=0, tiled=True)  32.5 us
    pallas_call x2, Pallas kernels, turn(): pl.pallas_call(lambda *refs: turn_kernel(plan, *refs), out_shape=(residua...  23.5 us
    pallas_call x4, Pallas kernels, grid(): pl.pallas_call(lambda *refs: grid_kernel(plan, not kept, lvl, g * columns...  13.7 us
    pallas_call x4, Pallas kernels, collected(): pl.pallas_call(lambda *refs: collect_kernel(here, quantities, *refs), out...  12.3 us
    pallas_call x2, Pallas kernels, last(): pl.pallas_call(lambda *refs: last_kernel(plan, *refs), out_shape=(shape(*...  8.85 us
  transfers between devices with their start and end apart: 16, of which 9 were waited for; matrix products, arithmetic and copies ran while one was open for 0% of the time, Pallas kernels for 19%

profile of v2, /device:TPU:0, one launch (start us, length us, event | category | flops | bytes accessed | tf_op | source)
XLA Modules:
  0.0 271.1 jit_solution(3020091775430558221)
XLA Ops:
  1.4 1.6 copy-done
  3.0 1.6 copy-done.2
  4.5 2.6 shard_map.96
  8.2 6.4 %all-to-all-start.1 = ((bf16[16,288,128]{2,1,0:T(8,128)(2,1)}), bf16[16,288,128]{2,1,0:T(8,128)(2,1)S(1)}, u32[]{:S(2)}, u32[]{:S(2)}) async-start(bf16[16,288,128]{2,1,0:T(8,128)(2,1)} %copy-done.11), calls=%async_computation.1 | async-start | bytes 2359296 | tf_op jit(solution)/shard_map/all_to_all | solution.py:397
  14.7 2.7 collective-permute-start
  17.3 11.3 %collective-permute-done.refs_3_ = bf16[32,128]{1,0:T(8,128)(2,1)S(1)} collective-permute-done((bf16[32,128]{1,0:T(8,128)(2,1)S(1)}, bf16[32,128]{1,0:T(8,128)(2,1)S(1)}, u32[]{:S(2)}, u32[]{:S(2)}) %collective-permute-start) | collective-permute-done | bytes 8224 | tf_op jit(solution)/shard_map/ppermute | solution.py:400
  28.7 1.6 copy-done.3
  30.2 2.0 shard_map.95
  32.3 1.1 copy-done.10
  33.3 1.0 copy-done.8
  34.4 7.8 %all-to-all-start = ((bf16[16,336,128]{2,1,0:T(8,128)(2,1)}), bf16[16,336,128]{2,1,0:T(8,128)(2,1)S(1)}, u32[]{:S(2)}, u32[]{:S(2)}) async-start(bf16[16,336,128]{2,1,0:T(8,128)(2,1)} %copy-done.10), calls=%async_computation | async-start | bytes 2752512 | tf_op jit(solution)/shard_map/all_to_all | solution.py:397
  42.1 1.3 copy-done.9
  44.2 3.3 %shard_map.102.refs_3_ = bf16[1032,256]{1,0:T(8,128)(2,1)} custom-call(bf16[16,288,128]{2,1,0:T(8,128)(2,1)S(1)} %copy-done.9, s32[16,128]{1,0:T(8,128)S(1)} %get-tuple-element.20.refs_1_), custom_call_target="tpu_custom_call" | custom-call | tf_op jit(solution)/shard_map/pallas_call | solution.py:470
  47.5 1.8 collective-permute-start.4
  50.4 19.3 %all-to-all-done.refs_0_ = bf16[16,336,128]{2,1,0:T(8,128)(2,1)S(1)} async-done(((bf16[16,336,128]{2,1,0:T(8,128)(2,1)}), bf16[16,336,128]{2,1,0:T(8,128)(2,1)S(1)}, u32[]{:S(2)}, u32[]{:S(2)}) %all-to-all-start) | async-done | bytes 1376288 | tf_op jit(solution)/shard_map/all_to_all | solution.py:397
  69.8 4.7 %collective-permute-done.6.refs_4_ = bf16[1032,256]{1,0:T(8,128)(2,1)} collective-permute-done((bf16[1032,256]{1,0:T(8,128)(2,1)}, bf16[1032,256]{1,0:T(8,128)(2,1)}, u32[]{:S(2)}, u32[]{:S(2)}) %collective-permute-start.6) | collective-permute-done | bytes 528416 | tf_op jit(solution)/shard_map/ppermute | solution.py:400
  74.5 3.6 %shard_map.103 = (bf16[16,272,128]{2,1,0:T(8,128)(2,1)S(1)}, f32[1024,256]{1,0:T(8,128)S(1)}, f32[1,256]{1,0:T(1,128)S(1)}) custom-call(f32[8,8]{1,0:T(8,128)S(1)} %copy-done.42, f32[64]{0:T(128)S(1)} %copy-done.47, s32[3]{0:T(128)S(1)} %copy-done.48, bf16[1032,256]{1,0:T(8,128)(2,1)} %shard_map.102.refs_3_, ...), custom_call_target="tpu_custom_call" | custom-call | tf_op jit(solution)/shard_map/pallas_call | solution.py:481
  81.3 4.4 %all-to-all-start.5 = ((bf16[16,272,128]{2,1,0:T(8,128)(2,1)}), bf16[16,272,128]{2,1,0:T(8,128)(2,1)}, u32[]{:S(2)}, u32[]{:S(2)}) async-start(bf16[16,272,128]{2,1,0:T(8,128)(2,1)} %copy-done.23), calls=%async_computation.5 | async-start | bytes 2228224 | tf_op jit(solution)/shard_map/all_to_all | solution.py:397
  85.8 2.5 shard_map.97.refs_3_
  89.2 25.7 %collective-permute-done.1.refs_4_ = bf16[1032,256]{1,0:T(8,128)(2,1)S(1)} collective-permute-done((bf16[1032,256]{1,0:T(8,128)(2,1)S(1)}, bf16[1032,256]{1,0:T(8,128)(2,1)S(1)}, u32[]{:S(2)}, u32[]{:S(2)}) %collective-permute-start.1) | collective-permute-done | bytes 528416 | tf_op jit(solution)/shard_map/ppermute | solution.py:400
  114.8 3.3 %shard_map.98 = (bf16[16,272,128]{2,1,0:T(8,128)(2,1)S(1)}, f32[1024,256]{1,0:T(8,128)S(1)}, f32[1,256]{1,0:T(1,128)S(1)}) custom-call(f32[8,8]{1,0:T(8,128)S(1)} %copy-done.42, f32[64]{0:T(128)S(1)} %copy-done.47, s32[3]{0:T(128)S(1)} %copy-done.49, bf16[1032,256]{1,0:T(8,128)(2,1)S(1)} %shard_map.97.refs_3_, ...), custom_call_target="tpu_custom_call" | custom-call | tf_op jit(solution)/shard_map/pallas_call | solution.py:481
  120.7 3.9 %all-to-all-start.2 = ((bf16[16,272,128]{2,1,0:T(8,128)(2,1)}), bf16[16,272,128]{2,1,0:T(8,128)(2,1)S(1)}, u32[]{:S(2)}, u32[]{:S(2)}) async-start(bf16[16,272,128]{2,1,0:T(8,128)(2,1)} %copy-done.24), calls=%async_computation.2 | async-start | bytes 2228224 | tf_op jit(solution)/shard_map/all_to_all | solution.py:397
  124.7 1.6 copy-done.4
  126.3 12.4 %shard_map.104 = (f32[32,8192]{1,0:T(8,128)S(1)}, f32[32,128]{1,0:T(8,128)S(1)}, bf16[16,272,128]{2,1,0:T(8,128)(2,1)S(1)}) custom-call(bf16[16,272,128]{2,1,0:T(8,128)(2,1)} %all-to-all-done.5.refs_0_, f32[64,8192]{1,0:T(8,128)S(1)} %copy-done.1, bf16[128,64,128]{2,1,0:T(8,128)(2,1)S(1)} %copy-done.4, f32[64,1]{1,0:T(8,128)S(1)} %copy.13.refs_3_), custom_call_target="tpu_custom_call" | custom-call | tf_op jit(solution)/shard_map/pallas_call | solution.py:491
  139.7 1.0 copy-done.32
  141.4 5.0 %all-to-all-start.6 = ((bf16[16,272,128]{2,1,0:T(8,128)(2,1)}), bf16[16,272,128]{2,1,0:T(8,128)(2,1)}, u32[]{:S(2)}, u32[]{:S(2)}) async-start(bf16[16,272,128]{2,1,0:T(8,128)(2,1)} %copy-done.25), calls=%async_computation.6 | async-start | bytes 2228224 | tf_op jit(solution)/shard_map/all_to_all | solution.py:397
  146.5 1.6 copy-done.5
  148.1 11.1 %shard_map.99 = (f32[32,8192]{1,0:T(8,128)S(1)}, f32[32,128]{1,0:T(8,128)S(1)}, bf16[16,272,128]{2,1,0:T(8,128)(2,1)S(1)}) custom-call(bf16[16,272,128]{2,1,0:T(8,128)(2,1)S(1)} %all-to-all-done.2.refs_0_, f32[64,8192]{1,0:T(8,128)S(1)} %copy-done.1, bf16[128,64,128]{2,1,0:T(8,128)(2,1)S(1)} %copy-done.5, f32[64,1]{1,0:T(8,128)S(1)} %copy.13.refs_3_), custom_call_target="tpu_custom_call" | custom-call | tf_op jit(solution)/shard_map/pallas_call | solution.py:491
  161.2 2.2 all-to-all-done.6.refs_0_
  163.4 3.9 %all-to-all-start.3 = ((bf16[16,272,128]{2,1,0:T(8,128)(2,1)}), bf16[16,272,128]{2,1,0:T(8,128)(2,1)S(1)}, u32[]{:S(2)}, u32[]{:S(2)}) async-start(bf16[16,272,128]{2,1,0:T(8,128)(2,1)} %copy-done.22), calls=%async_computation.3 | async-start | bytes 2228224 | tf_op jit(solution)/shard_map/all_to_all | solution.py:397
  167.3 3.9 %shard_map.105.refs_3_ = bf16[1032,256]{1,0:T(8,128)(2,1)S(1)} custom-call(bf16[16,272,128]{2,1,0:T(8,128)(2,1)} %all-to-all-done.6.refs_0_, s32[16,128]{1,0:T(8,128)S(1)} %get-tuple-element.20.refs_1_), custom_call_target="tpu_custom_call" | custom-call | tf_op jit(solution)/shard_map/pallas_call | solution.py:470
  171.2 1.8 collective-permute-start.7
  173.1 24.5 %collective-permute-done.7.refs_4_ = bf16[1032,256]{1,0:T(8,128)(2,1)S(1)} collective-permute-done((bf16[1032,256]{1,0:T(8,128)(2,1)S(1)}, bf16[1032,256]{1,0:T(8,128)(2,1)S(1)}, u32[]{:S(2)}, u32[]{:S(2)}) %collective-permute-start.7) | collective-permute-done | bytes 528416 | tf_op jit(solution)/shard_map/ppermute | solution.py:400
  197.6 3.3 %shard_map.106 = bf16[16,272,128]{2,1,0:T(8,128)(2,1)S(1)} custom-call(f32[8,8]{1,0:T(8,128)S(1)} %copy-done.42, f32[64]{0:T(128)S(1)} %copy-done.47, s32[3]{0:T(128)S(1)} %copy-done.50, bf16[1032,256]{1,0:T(8,128)(2,1)S(1)} %shard_map.105.refs_3_, bf16[1032,256]{1,0:T(8,128)(2,1)S(1)} %collective-permute-done.7.refs_4_, bf16[8,64,128]{2,1,0:T(8,128)(2,1)S(1)} %copy-done.18, ...), custom_call_target="tpu_custom_call" | custom-call | tf_op jit(solution)/shard_map/pallas_call | solution.py:481
  202.9 4.0 %all-to-all-start.7 = ((bf16[16,272,128]{2,1,0:T(8,128)(2,1)}), bf16[16,272,128]{2,1,0:T(8,128)(2,1)S(1)}, u32[]{:S(2)}, u32[]{:S(2)}) async-start(bf16[16,272,128]{2,1,0:T(8,128)(2,1)} %copy-done.12), calls=%async_computation.7 | async-start | bytes 2228224 | tf_op jit(solution)/shard_map/all_to_all | solution.py:397
  207.0 1.2 copy-done.14
  208.2 2.6 shard_map.100.refs_3_
  210.8 2.8 %collective-permute-start.5 = (bf16[1032,256]{1,0:T(8,128)(2,1)S(1)}, bf16[1032,256]{1,0:T(8,128)(2,1)S(1)}, u32[]{:S(2)}, u32[]{:S(2)}) collective-permute-start(bf16[1032,256]{1,0:T(8,128)(2,1)S(1)} %shard_map.100.refs_3_), channel_id=1, source_target_pairs={{0,16},{16,0},{1,17},{17,1},{2,18},{18,2},{3,19},{19,3},{4,20},{20... | collective-permute-start | bytes 1585160 | tf_op jit(solution)/shard_map/ppermute | solution.py:400
  213.6 23.9 %collective-permute-done.5.refs_4_ = bf16[1032,256]{1,0:T(8,128)(2,1)S(1)} collective-permute-done((bf16[1032,256]{1,0:T(8,128)(2,1)S(1)}, bf16[1032,256]{1,0:T(8,128)(2,1)S(1)}, u32[]{:S(2)}, u32[]{:S(2)}) %collective-permute-start.5) | collective-permute-done | bytes 528416 | tf_op jit(solution)/shard_map/ppermute | solution.py:400
  237.5 3.4 %shard_map.101 = bf16[16,272,128]{2,1,0:T(8,128)(2,1)S(1)} custom-call(f32[8,8]{1,0:T(8,128)S(1)} %copy-done.42, f32[64]{0:T(128)S(1)} %copy-done.47, s32[3]{0:T(128)S(1)} %copy-done.51, bf16[1032,256]{1,0:T(8,128)(2,1)S(1)} %shard_map.100.refs_3_, bf16[1032,256]{1,0:T(8,128)(2,1)S(1)} %collective-permute-done.5.refs_4_, bf16[8,64,128]{2,1,0:T(8,128)(2,1)S(1)} %copy-done.18, ...), custom_call_target="tpu_custom_call" | custom-call | tf_op jit(solution)/shard_map/pallas_call | solution.py:481
  241.8 4.5 %all-to-all-start.4 = ((bf16[16,272,128]{2,1,0:T(8,128)(2,1)}), bf16[16,272,128]{2,1,0:T(8,128)(2,1)}, u32[]{:S(2)}, u32[]{:S(2)}) async-start(bf16[16,272,128]{2,1,0:T(8,128)(2,1)} %copy-done.15), calls=%async_computation.4 | async-start | bytes 2228224 | tf_op jit(solution)/shard_map/all_to_all | solution.py:397
  246.4 1.6 copy-done.6
  248.0 1.2 copy-done.33
  249.2 3.8 %shard_map.107 = (f32[64,8192]{1,0:T(8,128)}, f32[64,8192]{1,0:T(8,128)}) custom-call(bf16[16,272,128]{2,1,0:T(8,128)(2,1)S(1)} %all-to-all-done.7.refs_0_, f32[64,8192]{1,0:T(8,128)S(1)} %copy-done.1, bf16[128,64,128]{2,1,0:T(8,128)(2,1)S(1)} %copy-done.6, f32[64,1]{1,0:T(8,128)S(1)} %copy-done.41, f32[32,8192]{1,0:T(8,128)S(1)} %copy-done.33, ...), custom_call_target="tpu_custom_call" | custom-call | tf_op jit(solution)/shard_map/pallas_call | solution.py:502
  253.0 10.2 %all-to-all-done.4.refs_0_ = bf16[16,272,128]{2,1,0:T(8,128)(2,1)} async-done(((bf16[16,272,128]{2,1,0:T(8,128)(2,1)}), bf16[16,272,128]{2,1,0:T(8,128)(2,1)}, u32[]{:S(2)}, u32[]{:S(2)}) %all-to-all-start.4) | async-done | bytes 1114144 | tf_op jit(solution)/shard_map/all_to_all | solution.py:397
  263.2 1.6 copy-done.7
  264.8 1.2 copy-done.39
  266.0 5.0 %shard_map.108 = (f32[64,8192]{1,0:T(8,128)}, f32[64,8192]{1,0:T(8,128)}) custom-call(bf16[16,272,128]{2,1,0:T(8,128)(2,1)} %all-to-all-done.4.refs_0_, f32[64,8192]{1,0:T(8,128)S(1)} %copy-done.1, bf16[128,64,128]{2,1,0:T(8,128)(2,1)S(1)} %copy-done.7, f32[64,1]{1,0:T(8,128)S(1)} %copy-done.41, ...), custom_call_target="tpu_custom_call", output_to_operand_aliasing={{0}: (6, {}), {1}: (7, {})} | custom-call | tf_op jit(solution)/shard_map/pallas_call | solution.py:502
  (120 shorter events, 17.2 us)
Async XLA Ops:
  1.4 1.6 copy-start
  8.2 6.5 %copy-start.56 = (bf16[16,2,128]{2,1,0:T(2,128)(2,1)S(1)}, bf16[16,2,128]{2,1,0:T(2,128)(2,1)}, u32[]{:S(2)}) copy-start(bf16[16,2,128]{2,1,0:T(2,128)(2,1)} %param.12) | copy-start | bytes 24580
  8.2 20.5 %copy-start.1 = (f32[64,8192]{1,0:T(8,128)S(1)}, f32[64,8192]{1,0:T(8,128)}, u32[]{:S(2)}) copy-start(f32[64,8192]{1,0:T(8,128)} %refs_1_.19) | copy-start | bytes 6291460
  8.2 25.2 %all-to-all-start.1 = ((bf16[16,288,128]{2,1,0:T(8,128)(2,1)}), bf16[16,288,128]{2,1,0:T(8,128)(2,1)S(1)}, u32[]{:S(2)}, u32[]{:S(2)}) async-start(bf16[16,288,128]{2,1,0:T(8,128)(2,1)} %copy-done.11), calls=%async_computation.1 | async-start | bytes 2359296 | tf_op jit(solution)/shard_map/all_to_all | solution.py:397
  14.7 14.0 %collective-permute-start = (bf16[32,128]{1,0:T(8,128)(2,1)S(1)}, bf16[32,128]{1,0:T(8,128)(2,1)S(1)}, u32[]{:S(2)}, u32[]{:S(2)}) collective-permute-start(bf16[32,128]{1,0:T(8,128)(2,1)S(1)} %bitcast.24), channel_id=1, source_target_pairs={{0,16},{16,0},{1,17},{17,1},{2,18},{18,2},{3,19},{19,3},{4,20},{20... | collective-permute-start | bytes 24584 | tf_op jit(solution)/shard_map/ppermute | solution.py:400
  28.7 1.6 copy-start.3
  34.4 35.3 %all-to-all-start = ((bf16[16,336,128]{2,1,0:T(8,128)(2,1)}), bf16[16,336,128]{2,1,0:T(8,128)(2,1)S(1)}, u32[]{:S(2)}, u32[]{:S(2)}) async-start(bf16[16,336,128]{2,1,0:T(8,128)(2,1)} %copy-done.10), calls=%async_computation | async-start | bytes 2752512 | tf_op jit(solution)/shard_map/all_to_all | solution.py:397
  44.1 3.3 %copy-start.26 = (bf16[2,128,128]{2,1,0:T(8,128)(2,1)S(1)}, bf16[2,128,128]{2,1,0:T(8,128)(2,1)}, u32[]{:S(2)}) copy-start(bf16[2,128,128]{2,1,0:T(8,128)(2,1)} %refs_8_.7) | copy-start | bytes 196612
  47.4 27.0 %copy-start.42 = (f32[8,8]{1,0:T(8,128)S(1)}, f32[8,8]{1,0:T(8,128)}, u32[]{:S(2)}) copy-start(f32[8,8]{1,0:T(8,128)} %refs_0_.11) | copy-start | bytes 772
  47.4 27.0 %copy-start.47 = (f32[64]{0:T(128)S(1)}, f32[64]{0:T(128)}, u32[]{:S(2)}) copy-start(f32[64]{0:T(128)} %refs_1_.17) | copy-start | bytes 772
  47.4 27.0 %collective-permute-start.6 = (bf16[1032,256]{1,0:T(8,128)(2,1)}, bf16[1032,256]{1,0:T(8,128)(2,1)}, u32[]{:S(2)}, u32[]{:S(2)}) collective-permute-start(bf16[1032,256]{1,0:T(8,128)(2,1)} %shard_map.102.refs_3_), channel_id=1, source_target_pairs={{0,16},{16,0},{1,17},{17,1},{2,18},{18,2},{3,19},{19,3},{4,20},{20... | collective-permute-start | bytes 1585160 | tf_op jit(solution)/shard_map/ppermute | solution.py:400
  47.5 22.3 %collective-permute-start.4 = (bf16[2,128,128]{2,1,0:T(8,128)(2,1)S(1)}, bf16[2,128,128]{2,1,0:T(8,128)(2,1)}, u32[]{:S(2)}, u32[]{:S(2)}) collective-permute-start(bf16[2,128,128]{2,1,0:T(8,128)(2,1)S(1)} %copy-done.26), channel_id=1, source_target_pairs={{0,3},{1,0},{2,1},{3,2},{4,7},{5,4},{6,5},{7,6},{8,11},{9,8},{10,9... | collective-permute-start | bytes 196616 | tf_op jit(solution)/shard_map/ppermute | solution.py:519
  49.2 20.5 %collective-permute-start.3 = (bf16[2,128,128]{2,1,0:T(8,128)(2,1)S(1)}, bf16[2,128,128]{2,1,0:T(8,128)(2,1)}, u32[]{:S(2)}, u32[]{:S(2)}) collective-permute-start(bf16[2,128,128]{2,1,0:T(8,128)(2,1)S(1)} %copy-done.26), channel_id=1, source_target_pairs={{0,2},{1,3},{2,0},{3,1},{4,6},{5,7},{6,4},{7,5},{8,10},{9,11},{10,... | collective-permute-start | bytes 196616 | tf_op jit(solution)/shard_map/ppermute | solution.py:519
  49.6 20.1 %collective-permute-start.2 = (bf16[2,128,128]{2,1,0:T(8,128)(2,1)S(1)}, bf16[2,128,128]{2,1,0:T(8,128)(2,1)}, u32[]{:S(2)}, u32[]{:S(2)}) collective-permute-start(bf16[2,128,128]{2,1,0:T(8,128)(2,1)S(1)} %copy-done.26), channel_id=1, source_target_pairs={{0,1},{1,2},{2,3},{3,0},{4,5},{5,6},{6,7},{7,4},{8,9},{9,10},{10,1... | collective-permute-start | bytes 196616 | tf_op jit(solution)/shard_map/ppermute | solution.py:519
  69.7 4.7 %copy-start.28 = (s32[128,128]{1,0:T(8,128)S(1)}, s32[128,128]{1,0:T(8,128)}, u32[]{:S(2)}) copy-start(s32[128,128]{1,0:T(8,128)} %copy-done.27) | copy-start | bytes 196612
  69.7 4.7 %copy-start.48 = (s32[3]{0:T(128)S(1)}, s32[3]{0:T(128)}, u32[]{:S(2)}) copy-start(s32[3]{0:T(128)} %pad_add_fusion.refs_2_) | copy-start | bytes 40
  69.7 8.4 %copy-start.19 = (bf16[8,64,128]{2,1,0:T(8,128)(2,1)}, bf16[8,64,128]{2,1,0:T(8,128)(2,1)S(1)}, u32[]{:S(2)}) copy-start(bf16[8,64,128]{2,1,0:T(8,128)(2,1)S(1)} %get-tuple-element.22.refs_6_) | copy-start | bytes 393220
  81.3 39.4 %all-to-all-start.5 = ((bf16[16,272,128]{2,1,0:T(8,128)(2,1)}), bf16[16,272,128]{2,1,0:T(8,128)(2,1)}, u32[]{:S(2)}, u32[]{:S(2)}) async-start(bf16[16,272,128]{2,1,0:T(8,128)(2,1)} %copy-done.23), calls=%async_computation.5 | async-start | bytes 2228224 | tf_op jit(solution)/shard_map/all_to_all | solution.py:397
  85.7 29.1 %copy-start.17 = (bf16[8,64,128]{2,1,0:T(8,128)(2,1)S(1)}, bf16[8,64,128]{2,1,0:T(8,128)(2,1)}, u32[]{:S(2)}) copy-start(bf16[8,64,128]{2,1,0:T(8,128)(2,1)} %copy-done.16) | copy-start | bytes 393220
  85.7 29.1 %copy-start.20 = (bf16[8,64,128]{2,1,0:T(8,128)(2,1)S(1)}, bf16[8,64,128]{2,1,0:T(8,128)(2,1)}, u32[]{:S(2)}) copy-start(bf16[8,64,128]{2,1,0:T(8,128)(2,1)} %copy-done.19) | copy-start | bytes 393220
  85.7 29.1 %copy-start.29 = (s32[128,128]{1,0:T(8,128)S(1)}, s32[128,128]{1,0:T(8,128)}, u32[]{:S(2)}) copy-start(s32[128,128]{1,0:T(8,128)} %copy-done.27) | copy-start | bytes 196612
  85.8 29.1 %copy-start.49 = (s32[3]{0:T(128)S(1)}, s32[3]{0:T(128)}, u32[]{:S(2)}) copy-start(s32[3]{0:T(128)} %pad_add_fusion.refs_2_) | copy-start | bytes 40
  88.3 26.6 %collective-permute-start.1 = (bf16[1032,256]{1,0:T(8,128)(2,1)S(1)}, bf16[1032,256]{1,0:T(8,128)(2,1)S(1)}, u32[]{:S(2)}, u32[]{:S(2)}) collective-permute-start(bf16[1032,256]{1,0:T(8,128)(2,1)S(1)} %shard_map.97.refs_3_), channel_id=1, source_target_pairs={{0,16},{16,0},{1,17},{17,1},{2,18},{18,2},{3,19},{19,3},{4,20},{20... | collective-permute-start | bytes 1585160 | tf_op jit(solution)/shard_map/ppermute | solution.py:400
  120.7 20.7 %all-to-all-start.2 = ((bf16[16,272,128]{2,1,0:T(8,128)(2,1)}), bf16[16,272,128]{2,1,0:T(8,128)(2,1)S(1)}, u32[]{:S(2)}, u32[]{:S(2)}) async-start(bf16[16,272,128]{2,1,0:T(8,128)(2,1)} %copy-done.24), calls=%async_computation.2 | async-start | bytes 2228224 | tf_op jit(solution)/shard_map/all_to_all | solution.py:397
  126.3 20.2 %copy-start.40 = (f32[64,1]{1,0:T(8,128)}, f32[64,1]{1,0:T(8,128)S(1)}, u32[]{:S(2)}) copy-start(f32[64,1]{1,0:T(8,128)S(1)} %copy.13.refs_3_) | copy-start | bytes 772
  141.4 21.9 %all-to-all-start.6 = ((bf16[16,272,128]{2,1,0:T(8,128)(2,1)}), bf16[16,272,128]{2,1,0:T(8,128)(2,1)}, u32[]{:S(2)}, u32[]{:S(2)}) async-start(bf16[16,272,128]{2,1,0:T(8,128)(2,1)} %copy-done.25), calls=%async_computation.6 | async-start | bytes 2228224 | tf_op jit(solution)/shard_map/all_to_all | solution.py:397
  146.5 1.6 copy-start.5
  161.2 2.2 copy-start.45
  163.4 38.6 %all-to-all-start.3 = ((bf16[16,272,128]{2,1,0:T(8,128)(2,1)}), bf16[16,272,128]{2,1,0:T(8,128)(2,1)S(1)}, u32[]{:S(2)}, u32[]{:S(2)}) async-start(bf16[16,272,128]{2,1,0:T(8,128)(2,1)} %copy-done.22), calls=%async_computation.3 | async-start | bytes 2228224 | tf_op jit(solution)/shard_map/all_to_all | solution.py:397
  167.2 30.3 %copy-start.18 = (bf16[8,64,128]{2,1,0:T(8,128)(2,1)S(1)}, bf16[8,64,128]{2,1,0:T(8,128)(2,1)}, u32[]{:S(2)}) copy-start(bf16[8,64,128]{2,1,0:T(8,128)(2,1)} %copy-done.16) | copy-start | bytes 393220
  167.3 30.3 %copy-start.21 = (bf16[8,64,128]{2,1,0:T(8,128)(2,1)S(1)}, bf16[8,64,128]{2,1,0:T(8,128)(2,1)}, u32[]{:S(2)}) copy-start(bf16[8,64,128]{2,1,0:T(8,128)(2,1)} %copy-done.19) | copy-start | bytes 393220
  167.3 30.3 %copy-start.30 = (s32[128,128]{1,0:T(8,128)S(1)}, s32[128,128]{1,0:T(8,128)}, u32[]{:S(2)}) copy-start(s32[128,128]{1,0:T(8,128)} %copy-done.27) | copy-start | bytes 196612
  167.3 30.3 %copy-start.37 = (f32[1024,256]{1,0:T(8,128)S(1)}, f32[1024,256]{1,0:T(8,128)}, u32[]{:S(2)}) copy-start(f32[1024,256]{1,0:T(8,128)} %copy-done.36) | copy-start | bytes 3145732
  167.3 30.3 %copy-start.50 = (s32[3]{0:T(128)S(1)}, s32[3]{0:T(128)}, u32[]{:S(2)}) copy-start(s32[3]{0:T(128)} %pad_add_fusion.refs_2_) | copy-start | bytes 40
  167.3 30.3 %copy-start.55 = (f32[1,256]{1,0:T(1,128)S(1)}, f32[1,256]{1,0:T(1,128)}, u32[]{:S(2)}) copy-start(f32[1,256]{1,0:T(1,128)} %copy-done.54) | copy-start | bytes 3076
  171.2 26.3 %collective-permute-start.7 = (bf16[1032,256]{1,0:T(8,128)(2,1)S(1)}, bf16[1032,256]{1,0:T(8,128)(2,1)S(1)}, u32[]{:S(2)}, u32[]{:S(2)}) collective-permute-start(bf16[1032,256]{1,0:T(8,128)(2,1)S(1)} %shard_map.105.refs_3_), channel_id=1, source_target_pairs={{0,16},{16,0},{1,17},{17,1},{2,18},{18,2},{3,19},{19,3},{4,20},{20... | collective-permute-start | bytes 1585160 | tf_op jit(solution)/shard_map/ppermute | solution.py:400
  202.9 38.9 %all-to-all-start.7 = ((bf16[16,272,128]{2,1,0:T(8,128)(2,1)}), bf16[16,272,128]{2,1,0:T(8,128)(2,1)S(1)}, u32[]{:S(2)}, u32[]{:S(2)}) async-start(bf16[16,272,128]{2,1,0:T(8,128)(2,1)} %copy-done.12), calls=%async_computation.7 | async-start | bytes 2228224 | tf_op jit(solution)/shard_map/all_to_all | solution.py:397
  208.2 29.2 %copy-start.31 = (s32[128,128]{1,0:T(8,128)S(1)}, s32[128,128]{1,0:T(8,128)}, u32[]{:S(2)}) copy-start(s32[128,128]{1,0:T(8,128)} %copy-done.27) | copy-start | bytes 196612
  208.2 29.2 %copy-start.35 = (f32[1024,256]{1,0:T(8,128)S(1)}, f32[1024,256]{1,0:T(8,128)}, u32[]{:S(2)}) copy-start(f32[1024,256]{1,0:T(8,128)} %copy-done.34) | copy-start | bytes 3145732
  208.2 29.2 %copy-start.51 = (s32[3]{0:T(128)S(1)}, s32[3]{0:T(128)}, u32[]{:S(2)}) copy-start(s32[3]{0:T(128)} %pad_add_fusion.refs_2_) | copy-start | bytes 40
  208.2 29.2 %copy-start.53 = (f32[1,256]{1,0:T(1,128)S(1)}, f32[1,256]{1,0:T(1,128)}, u32[]{:S(2)}) copy-start(f32[1,256]{1,0:T(1,128)} %copy-done.52) | copy-start | bytes 3076
  210.8 26.6 %collective-permute-start.5 = (bf16[1032,256]{1,0:T(8,128)(2,1)S(1)}, bf16[1032,256]{1,0:T(8,128)(2,1)S(1)}, u32[]{:S(2)}, u32[]{:S(2)}) collective-permute-start(bf16[1032,256]{1,0:T(8,128)(2,1)S(1)} %shard_map.100.refs_3_), channel_id=1, source_target_pairs={{0,16},{16,0},{1,17},{17,1},{2,18},{18,2},{3,19},{19,3},{4,20},{20... | collective-permute-start | bytes 1585160 | tf_op jit(solution)/shard_map/ppermute | solution.py:400
  241.8 4.5 %copy-start.41 = (f32[64,1]{1,0:T(8,128)S(1)}, f32[64,1]{1,0:T(8,128)}, u32[]{:S(2)}) copy-start(f32[64,1]{1,0:T(8,128)} %copy-done.40) | copy-start | bytes 772
  241.8 4.5 %copy-start.44 = (f32[32,128]{1,0:T(8,128)S(1)}, f32[32,128]{1,0:T(8,128)}, u32[]{:S(2)}) copy-start(f32[32,128]{1,0:T(8,128)} %copy-done.43) | copy-start | bytes 49156
  241.8 21.4 %all-to-all-start.4 = ((bf16[16,272,128]{2,1,0:T(8,128)(2,1)}), bf16[16,272,128]{2,1,0:T(8,128)(2,1)}, u32[]{:S(2)}, u32[]{:S(2)}) async-start(bf16[16,272,128]{2,1,0:T(8,128)(2,1)} %copy-done.15), calls=%async_computation.4 | async-start | bytes 2228224 | tf_op jit(solution)/shard_map/all_to_all | solution.py:397
  246.4 1.6 copy-start.6
  249.2 14.0 %copy-start.46 = (f32[32,128]{1,0:T(8,128)S(1)}, f32[32,128]{1,0:T(8,128)}, u32[]{:S(2)}) copy-start(f32[32,128]{1,0:T(8,128)} %copy-done.45) | copy-start | bytes 49156
  263.2 1.6 copy-start.7
  (25 other events, 25.3 us)
